TPU v7x, 32 devices: a whole 2x2x4 slice. The times are simulated.
32 devices in a mesh: tower: 2 (over core), blk: 8 (over z, x), seq: 2 (over y).
Axes of the slice: x: 2, y: 2, z: 4, core: 2. Of those that a mesh axis runs over, the one named last changes fastest.
Arguments:
- queries: bfloat16 [2, 2048, 1024], P('tower', ('blk', 'seq')), may hold values from -6 to 6
- key_rows: bfloat16 [2, 2048, 1024], P('tower', ('blk', 'seq')), may hold values from -6 to 6
- value_rows: bfloat16 [2, 2048, 1024], P('tower', ('blk', 'seq')), may hold values from -6 to 6
- cross_queries: bfloat16 [2, 2048, 1024], P('tower', ('blk', 'seq')), may hold values from -6 to 6
- cross_keys: bfloat16 [2, 2048, 1024], P('tower', ('blk', 'seq')), may hold values from -6 to 6
- cross_values: bfloat16 [2, 2048, 1024], P('tower', ('blk', 'seq')), may hold values from -6 to 6
- grad_out: bfloat16 [2, 2048, 1024], P('tower', ('blk', 'seq')), may hold values from -6 to 6
- offsets: int32 [2, 8], replicated, may hold values from -127 to 127, as said below
- key_valid: int32 [2, 2048], P(None, ('blk', 'seq')), may hold values from 0 to 1, as said below
Outputs:
- attended: bfloat16 [2, 2048, 1024], P('tower', ('blk', 'seq'))
- grad_queries: bfloat16 [2, 2048, 1024], P('tower', ('blk', 'seq'))
- grad_keys: bfloat16 [2, 2048, 1024], P('tower', ('blk', 'seq'))
- grad_values: bfloat16 [2, 2048, 1024], P('tower', ('blk', 'seq'))
- grad_cross_queries: bfloat16 [2, 2048, 1024], P('tower', ('blk', 'seq'))
- grad_cross_keys: bfloat16 [2, 2048, 1024], P('tower', ('blk', 'seq'))
- grad_cross_values: bfloat16 [2, 2048, 1024], P('tower', ('blk', 'seq'))
Inputs may be any that keep to these rules, and one draw needn't show every extreme that they name: Both ends of the range occur in every draw; for every block b, offsets[0, b] and offsets[1, b] have opposite signs, and every magnitude is at least 64. `key_valid`: positions k * 256 + 256 // 2 - 1 and k * 256 + 256 // 2 are always 1.
All inputs are finite; a program needn't handle non-finite values.
Results may differ from a plain program's by a relative error of at most 0.019.
Values may be sent and summed in bfloat16 or wider, within the bound.
A program may use at most 128 MiB of HBM per device.

v0:
```python
import jax
import jax.numpy as jnp
from jax import lax
from jax.sharding import PartitionSpec as P

HEADS = 16
HEAD = 64
WINDOW = 2048
TILE = 512


def extended(block, sides, width):
    for axis, dim in sides:
        count = lax.axis_size(axis)
        forward = [(i, i + 1) for i in range(count - 1)]
        backward = [(target, source) for source, target in forward]
        low = lax.ppermute(
            lax.slice_in_dim(block, block.shape[dim] - width, None, axis=dim), axis, forward
        )
        high = lax.ppermute(lax.slice_in_dim(block, 0, width, axis=dim), axis, backward)
        block = jnp.concatenate([low, block, high], axis=dim)
    return block


def swapped(value, axis, bit):
    mask = 2**bit
    pairs = [(source, source ^ mask) for source in range(lax.axis_size(axis))]
    return lax.ppermute(value, axis, pairs)


def passed_along(block, axis, distance):
    devices = range(lax.axis_size(axis))
    route = [(i - distance, i) for i in devices if i - distance in devices]
    return lax.ppermute(block, axis, route)


def attend(query_tile, grad_tile, key_block, value_block, allowed, heads_here):
    score_scale = HEAD ** (-0.5)
    rows_count = query_tile.shape[0]
    keys_count = key_block.shape[0]
    q_heads = query_tile.reshape(rows_count, heads_here, HEAD)
    g_heads = grad_tile.reshape(rows_count, heads_here, HEAD)
    k_heads = key_block.reshape(keys_count, heads_here, HEAD)
    v_heads = value_block.reshape(keys_count, heads_here, HEAD)
    scores = (
        jnp.einsum("qhe,khe->hqk", q_heads, k_heads, preferred_element_type=jnp.float32)
        * score_scale
    )
    scores = jnp.where(allowed[None], scores, -1e30)
    row_max = jnp.max(scores, axis=2)
    unnormed = jnp.exp(scores - row_max[:, :, None])
    row_sum = jnp.sum(unnormed, axis=2)
    weights = unnormed / row_sum[:, :, None]
    prob_bf = weights.astype(jnp.bfloat16)
    result = jnp.einsum(
        "hqk,khe->qhe", prob_bf, v_heads, preferred_element_type=jnp.float32
    ).reshape(rows_count, -1)
    grad_probs = jnp.einsum("qhe,khe->hqk", g_heads, v_heads, preferred_element_type=jnp.float32)
    row_dot = jnp.sum(weights * grad_probs, axis=2)
    grad_scores = (weights * (grad_probs - row_dot[:, :, None]) * score_scale).astype(jnp.bfloat16)
    grad_query = jnp.einsum(
        "hqk,khe->qhe", grad_scores, k_heads, preferred_element_type=jnp.float32
    ).reshape(rows_count, -1)
    grad_key = jnp.einsum(
        "hqk,qhe->khe", grad_scores, q_heads, preferred_element_type=jnp.float32
    ).reshape(keys_count, -1)
    grad_value = jnp.einsum(
        "hqk,qhe->khe", prob_bf, g_heads, preferred_element_type=jnp.float32
    ).reshape(keys_count, -1)
    return (result, grad_query, grad_key, grad_value, jnp.stack((row_max, row_sum, row_dot)))


def shards(
    queries,
    key_rows,
    value_rows,
    cross_queries,
    cross_keys,
    cross_values,
    grad_out,
    offsets,
    key_valid,
):
    seq_count = lax.axis_size("seq")
    heads_here = HEADS // seq_count
    local_rows = (
        queries[0],
        key_rows[0],
        value_rows[0],
        cross_queries[0],
        cross_keys[0],
        cross_values[0],
        grad_out[0],
    )
    query_here, key_here, value_here, cross_query, cross_key, cross_value, cotangent = (
        lax.all_to_all(local_rows[0], "seq", split_axis=1, concat_axis=0, tiled=True),
        lax.all_to_all(local_rows[1], "seq", split_axis=1, concat_axis=0, tiled=True),
        lax.all_to_all(local_rows[2], "seq", split_axis=1, concat_axis=0, tiled=True),
        lax.all_to_all(local_rows[3], "seq", split_axis=1, concat_axis=0, tiled=True),
        lax.all_to_all(local_rows[4], "seq", split_axis=1, concat_axis=0, tiled=True),
        lax.all_to_all(local_rows[5], "seq", split_axis=1, concat_axis=0, tiled=True),
        lax.all_to_all(local_rows[6], "seq", split_axis=1, concat_axis=0, tiled=True),
    )
    block_len = query_here.shape[0]
    columns = query_here.shape[1]
    half_width = min(WINDOW // 2, block_len // 2)
    tile_rows = min(TILE, block_len)
    tile_count = block_len // tile_rows
    window_span = tile_rows + 2 * half_width
    tower_id = lax.axis_index("tower")
    block_id = lax.axis_index("blk")
    block_mask = lax.all_gather(key_valid, "seq", axis=1, tiled=True)
    mask_ext = extended(block_mask, (("blk", 1),), half_width)
    self_valid = lax.dynamic_index_in_dim(mask_ext, tower_id, 0, keepdims=False)
    other_valid = lax.dynamic_index_in_dim(mask_ext, 1 - tower_id, 0, keepdims=False)
    pair_ext = extended(jnp.stack((key_here, value_here)), (("blk", 1),), half_width)
    partner = swapped(jnp.stack((cross_key, cross_value)), "tower", 0)
    partner_ext = extended(partner, (("blk", 1),), half_width)
    align_shift = offsets[tower_id, block_id]
    band_start = half_width + align_shift
    band = lax.dynamic_slice_in_dim(partner_ext, band_start, block_len, 1)
    band_valid = lax.dynamic_slice_in_dim(other_valid, band_start, block_len) > 0
    rows_local = jnp.arange(tile_rows)
    keys_local = jnp.arange(window_span)
    near = jnp.abs(rows_local[:, None] + half_width - keys_local[None, :]) <= half_width

    def self_step(carry, tile_index):
        grad_key_acc, grad_value_acc = carry
        tile_start = tile_index * tile_rows
        query_tile = lax.dynamic_slice_in_dim(query_here, tile_start, tile_rows, 0)
        grad_tile = lax.dynamic_slice_in_dim(cotangent, tile_start, tile_rows, 0)
        key_window = lax.dynamic_slice_in_dim(pair_ext[0], tile_start, window_span, 0)
        value_window = lax.dynamic_slice_in_dim(pair_ext[1], tile_start, window_span, 0)
        allowed = (
            near & (lax.dynamic_slice_in_dim(self_valid, tile_start, window_span) > 0)[None, :]
        )
        result, grad_query, grad_key, grad_value, stats = attend(
            query_tile, grad_tile, key_window, value_window, allowed, heads_here
        )
        grad_key_acc = lax.dynamic_update_slice_in_dim(
            grad_key_acc,
            lax.dynamic_slice_in_dim(grad_key_acc, tile_start, window_span, 0) + grad_key,
            tile_start,
            0,
        )
        grad_value_acc = lax.dynamic_update_slice_in_dim(
            grad_value_acc,
            lax.dynamic_slice_in_dim(grad_value_acc, tile_start, window_span, 0) + grad_value,
            tile_start,
            0,
        )
        return ((grad_key_acc, grad_value_acc), (result, grad_query, stats))

    def cross_step(carry, tile_index):
        grad_key_acc, grad_value_acc = carry
        tile_start = tile_index * tile_rows
        query_tile = lax.dynamic_slice_in_dim(cross_query, tile_start, tile_rows, 0)
        grad_tile = lax.dynamic_slice_in_dim(cotangent, tile_start, tile_rows, 0)
        result, grad_query, grad_key, grad_value, stats = attend(
            query_tile, grad_tile, band[0], band[1], band_valid[None, :], heads_here
        )
        return ((grad_key_acc + grad_key, grad_value_acc + grad_value), (result, grad_query))

    zeros_ext = jnp.zeros((block_len + 2 * half_width, columns), jnp.float32)
    zeros_band = jnp.zeros((block_len, columns), jnp.float32)
    tile_ids = jnp.arange(tile_count)
    (self_gk, self_gv), (self_out, self_gq, self_stats) = lax.scan(
        self_step, (zeros_ext, zeros_ext), tile_ids
    )
    (cross_gk, cross_gv), (cross_out, cross_gq) = lax.scan(
        cross_step, (zeros_band, zeros_band), tile_ids
    )
    self_out = self_out.reshape(block_len, columns)
    cross_out = cross_out.reshape(block_len, columns)
    self_stats = jnp.transpose(self_stats, (1, 2, 0, 3)).reshape(3, heads_here, block_len)
    attended = (self_out + cross_out).astype(jnp.bfloat16)
    cross_ext = jnp.zeros((2, block_len + 2 * half_width, columns), jnp.float32)
    cross_ext = lax.dynamic_update_slice_in_dim(
        cross_ext, jnp.stack((cross_gk, cross_gv)), band_start, 1
    )
    self_ext = jnp.stack((self_gk, self_gv))
    self_core = self_ext[:, half_width : half_width + block_len]
    cross_core = cross_ext[:, half_width : half_width + block_len]
    upper_cut = block_len - half_width
    lower_send = jnp.concatenate((self_ext[:, :half_width], cross_ext[:, :half_width]), 0)
    upper_send = jnp.concatenate(
        (self_ext[:, block_len + half_width :], cross_ext[:, block_len + half_width :]), 0
    )
    from_above = passed_along(lower_send.astype(jnp.bfloat16), "blk", -1).astype(lower_send.dtype)
    from_below = passed_along(upper_send.astype(jnp.bfloat16), "blk", 1).astype(upper_send.dtype)
    self_core = (
        self_core.at[:, upper_cut:].add(from_above[:2]).at[:, :half_width].add(from_below[:2])
    )
    cross_core = (
        cross_core.at[:, upper_cut:].add(from_above[2:]).at[:, :half_width].add(from_below[2:])
    )
    returned = swapped(cross_core.astype(jnp.bfloat16), "tower", 0)
    head_outs = (
        attended,
        self_gq.reshape(block_len, columns).astype(jnp.bfloat16),
        self_core[0].astype(jnp.bfloat16),
        self_core[1].astype(jnp.bfloat16),
        cross_gq.reshape(block_len, columns).astype(jnp.bfloat16),
        returned[0],
        returned[1],
    )
    token_outs = (
        lax.all_to_all(head_outs[0], "seq", split_axis=0, concat_axis=1, tiled=True),
        lax.all_to_all(head_outs[1], "seq", split_axis=0, concat_axis=1, tiled=True),
        lax.all_to_all(head_outs[2], "seq", split_axis=0, concat_axis=1, tiled=True),
        lax.all_to_all(head_outs[3], "seq", split_axis=0, concat_axis=1, tiled=True),
        lax.all_to_all(head_outs[4], "seq", split_axis=0, concat_axis=1, tiled=True),
        lax.all_to_all(head_outs[5], "seq", split_axis=0, concat_axis=1, tiled=True),
        lax.all_to_all(head_outs[6], "seq", split_axis=0, concat_axis=1, tiled=True),
    )
    return tuple((piece[None] for piece in token_outs))


def solution(mesh):
    in_specs = (
        P("tower", ("blk", "seq"), None),
        P("tower", ("blk", "seq"), None),
        P("tower", ("blk", "seq"), None),
        P("tower", ("blk", "seq"), None),
        P("tower", ("blk", "seq"), None),
        P("tower", ("blk", "seq"), None),
        P("tower", ("blk", "seq"), None),
        P(),
        P(None, ("blk", "seq")),
    )
    out_specs = (
        P("tower", ("blk", "seq"), None),
        P("tower", ("blk", "seq"), None),
        P("tower", ("blk", "seq"), None),
        P("tower", ("blk", "seq"), None),
        P("tower", ("blk", "seq"), None),
        P("tower", ("blk", "seq"), None),
        P("tower", ("blk", "seq"), None),
    )
    return jax.shard_map(shards, mesh=mesh, in_specs=in_specs, out_specs=out_specs, check_vma=False)
```

profile of v0, /device:TPU:12, one launch (start us, length us, event | category | flops | bytes accessed | tf_op | source)
XLA Modules:
  0.0 235.8 jit_solution(7698826296991891058)
XLA Ops:
  0.7 1.8 copy.74
  2.5 4.1 %all-to-all-start.2 = ((bf16[128,2,512]{0,2,1:T(8,128)(2,1)}), bf16[128,2,512]{0,2,1:T(8,128)(2,1)S(1)}, u32[]{:S(2)}, u32[]{:S(2)}) async-start(bf16[128,2,512]{0,2,1:T(8,128)(2,1)} %bitcast.8), calls=%async_computation.2 | async-start | bytes 524288 | tf_op jit(solution)/shard_map/all_to_all | solution.py:96
  10.3 5.2 %all-to-all-start = ((bf16[128,2,512]{2,0,1:T(8,128)(2,1)}), bf16[128,2,512]{2,0,1:T(8,128)(2,1)S(1)}, u32[]{:S(2)}, u32[]{:S(2)}) async-start(bf16[128,2,512]{2,0,1:T(8,128)(2,1)} %copy.69), calls=%async_computation | async-start | bytes 524288 | tf_op jit(solution)/shard_map/all_to_all | solution.py:97
  16.5 2.1 all-to-all-done
  18.6 5.4 %all-to-all-start.1 = ((bf16[128,2,512]{2,0,1:T(8,128)(2,1)}), bf16[128,2,512]{2,0,1:T(8,128)(2,1)S(1)}, u32[]{:S(2)}, u32[]{:S(2)}) async-start(bf16[128,2,512]{2,0,1:T(8,128)(2,1)} %copy.71), calls=%async_computation.1 | async-start | bytes 524288 | tf_op jit(solution)/shard_map/all_to_all | solution.py:98
  24.9 4.2 %all_gather.3 = s32[2,256]{1,0:T(2,128)S(1)} all-gather(s32[2,128]{1,0:T(2,128)S(1)} %copy-done.15), channel_id=1, replica_groups=mesh['tower'=2,'blk'=8,'seq'=2] {'seq'}, dimensions={1}, use_global_device_ids=true | all-gather | bytes 3072 | tf_op jit(solution)/shard_map/all_gather | solution.py:112
  29.1 3.6 %all-to-all-start.5 = ((bf16[128,2,512]{0,2,1:T(8,128)(2,1)}), bf16[128,2,512]{0,2,1:T(8,128)(2,1)S(1)}, u32[]{:S(2)}, u32[]{:S(2)}) async-start(bf16[128,2,512]{0,2,1:T(8,128)(2,1)} %bitcast.21), calls=%async_computation.5 | async-start | bytes 524288 | tf_op jit(solution)/shard_map/all_to_all | solution.py:99
  32.7 3.3 %collective-permute-start.3 = (s32[2,128]{1,0:T(2,128)S(1)}, s32[2,128]{1,0:T(2,128)S(1)}, u32[]{:S(2)}, u32[]{:S(2)}) collective-permute-start(s32[2,128]{1,0:T(2,128)S(1)} %get-tuple-element.146), channel_id=1, source_target_pairs={{2,0},{4,2},{6,4},{8,6},{10,8},{12,10},{14,12},{3,1},{5,3},{7,5},{... | collective-permute-start | bytes 3080 | tf_op jit(solution)/shard_map/ppermute | solution.py:20
  36.0 2.6 %collective-permute-start.2 = (s32[2,128]{1,0:T(2,128)S(1)}, s32[2,128]{1,0:T(2,128)S(1)}, u32[]{:S(2)}, u32[]{:S(2)}) collective-permute-start(s32[2,128]{1,0:T(2,128)S(1)} %get-tuple-element.147), channel_id=1, source_target_pairs={{0,2},{2,4},{4,6},{6,8},{8,10},{10,12},{12,14},{1,3},{3,5},{5,7},{... | collective-permute-start | bytes 3080 | tf_op jit(solution)/shard_map/ppermute | solution.py:17
  43.4 3.5 %all-to-all-start.3 = ((bf16[128,2,512]{2,0,1:T(8,128)(2,1)}), bf16[128,2,512]{2,0,1:T(8,128)(2,1)S(1)}, u32[]{:S(2)}, u32[]{:S(2)}) async-start(bf16[128,2,512]{2,0,1:T(8,128)(2,1)} %copy.78), calls=%async_computation.3 | async-start | bytes 524288 | tf_op jit(solution)/shard_map/all_to_all | solution.py:100
  46.9 3.1 %all-to-all-done.3 = bf16[128,2,512]{2,0,1:T(8,128)(2,1)S(1)} async-done(((bf16[128,2,512]{2,0,1:T(8,128)(2,1)}), bf16[128,2,512]{2,0,1:T(8,128)(2,1)S(1)}, u32[]{:S(2)}, u32[]{:S(2)}) %all-to-all-start.3) | async-done | bytes 262176 | tf_op jit(solution)/shard_map/all_to_all | solution.py:100
  50.1 5.4 %all-to-all-start.4 = ((bf16[128,2,512]{2,0,1:T(8,128)(2,1)}), bf16[128,2,512]{2,0,1:T(8,128)(2,1)S(1)}, u32[]{:S(2)}, u32[]{:S(2)}) async-start(bf16[128,2,512]{2,0,1:T(8,128)(2,1)} %copy.80), calls=%async_computation.4 | async-start | bytes 524288 | tf_op jit(solution)/shard_map/all_to_all | solution.py:101
  56.0 4.3 %collective-permute-start = (bf16[2,128,512]{1,2,0:T(8,128)(2,1)S(1)}, bf16[2,128,512]{1,2,0:T(8,128)(2,1)}, u32[]{:S(2)}, u32[]{:S(2)}) collective-permute-start(bf16[2,128,512]{1,2,0:T(8,128)(2,1)S(1)} %get-tuple-element.140), channel_id=1, source_target_pairs={{0,2},{2,4},{4,6},{6,8},{8,10},{10,12},{12,14},{1,3},{3,5},{5,7},{... | collective-permute-start | bytes 786440 | tf_op jit(solution)/shard_map/ppermute | solution.py:17
  60.3 2.4 %collective-permute-start.1 = (bf16[2,128,512]{1,2,0:T(8,128)(2,1)S(1)}, bf16[2,128,512]{1,2,0:T(8,128)(2,1)}, u32[]{:S(2)}, u32[]{:S(2)}) collective-permute-start(bf16[2,128,512]{1,2,0:T(8,128)(2,1)S(1)} %get-tuple-element.141), channel_id=1, source_target_pairs={{2,0},{4,2},{6,4},{8,6},{10,8},{12,10},{14,12},{3,1},{5,3},{7,5},{... | collective-permute-start | bytes 786440 | tf_op jit(solution)/shard_map/ppermute | solution.py:20
  62.8 3.5 %all-to-all-start.7 = ((bf16[128,2,512]{0,2,1:T(8,128)(2,1)}), bf16[128,2,512]{0,2,1:T(8,128)(2,1)S(1)}, u32[]{:S(2)}, u32[]{:S(2)}) async-start(bf16[128,2,512]{0,2,1:T(8,128)(2,1)} %bitcast.27), calls=%async_computation.7 | async-start | bytes 524288 | tf_op jit(solution)/shard_map/all_to_all | solution.py:102
  71.3 2.8 %fusion.76 = f32[8,512,256]{2,1,0:T(8,128)} fusion(bf16[512,8,64]{0,2,1:T(8,128)(2,1)S(1)} %bitcast.178, bf16[256,8,64]{0,2,1:T(8,128)(2,1)S(1)} %reshape.328), kind=kOutput, calls=%fused_computation.111 | convolution fusion | flops 134217728 | bytes 4980736 | tf_op jit(solution)/shard_map/while/body/eval_jaxpr/qhe,khe->hqk/dot_general | solution.py:58
  74.1 3.5 %fusion.75 = (f32[8,256]{1,0:T(8,128)S(1)}, f32[8,256,512]{1,2,0:T(8,128)}) fusion(pred[256,512]{0,1:T(8,128)(4,1)S(1)} %fusion.48, bf16[512,8,64]{0,2,1:T(8,128)(2,1)S(1)} %bitcast.199, bf16[256,8,64]{0,2,1:T(8,128)(2,1)S(1)} %reshape.326), kind=kOutput, calls=%fused_computation.110 | convolution fusion | flops 138412544 | bytes 5120000 | tf_op jit(solution)/shard_map/while/body/eval_jaxpr/sub | solution.py:51
  77.5 7.3 %fusion.25 = bf16[256,8,64]{0,2,1:T(8,128)(2,1)S(1)} fusion(bf16[512,8,64]{0,2,1:T(8,128)(2,1)S(1)} %bitcast.200, f32[8,512,256]{2,1,0:T(8,128)} %fusion.76, f32[8,256,512]{1,2,0:T(8,128)} %get-tuple-element.151, f32[8,256]{1,0:T(8,128)S(1)} %get-tuple-element.150), kind=kOutput, calls=%fused_computation.40 | convolution fusion | flops 141691392 | bytes 9183232 | tf_op jit(solution)/shard_map/while/body/eval_jaxpr/hqk,khe->qhe/dot_general | solution.py:61
  84.8 7.2 %fusion.20 = f32[8,512,64]{1,2,0:T(8,128)S(1)} fusion(bf16[256,8,64]{0,2,1:T(8,128)(2,1)S(1)} %reshape.326, f32[8,512,256]{2,1,0:T(8,128)} %fusion.76, f32[8,256,512]{1,2,0:T(8,128)} %get-tuple-element.151, f32[8,256]{1,0:T(8,128)S(1)} %get-tuple-element.150), kind=kOutput, calls=%fused_computation.33 | convolution fusion | flops 141560320 | bytes 9707520 | tf_op jit(solution)/shard_map/while/body/eval_jaxpr/hqk,qhe->khe/dot_general | solution.py:64
  92.8 6.1 %all-to-all-start.8 = ((bf16[2,128,512]{1,2,0:T(8,128)(2,1)}), bf16[2,128,512]{1,2,0:T(8,128)(2,1)}, u32[]{:S(2)}, u32[]{:S(2)}) async-start(bf16[2,128,512]{1,2,0:T(8,128)(2,1)} %copy.91), calls=%async_computation.8 | async-start | bytes 524288 | tf_op jit(solution)/shard_map/all_to_all | solution.py:209
  98.9 2.9 %fusion.32 = f32[8,512,64]{1,2,0:T(8,128)S(1)} fusion(bf16[256,8,64]{0,2,1:T(8,128)(2,1)S(1)} %reshape.328, f32[8,256,512]{1,2,0:T(8,128)} %get-tuple-element.151, f32[8,256]{1,0:T(8,128)S(1)} %get-tuple-element.150), kind=kOutput, calls=%fused_computation.53 | convolution fusion | flops 136314880 | bytes 5513216 | tf_op jit(solution)/shard_map/while/body/eval_jaxpr/hqk,qhe->khe/dot_general | solution.py:67
  101.9 4.0 %collective-permute-start.6 = (bf16[2,128,512]{1,2,0:T(8,128)(2,1)S(1)}, bf16[2,128,512]{1,2,0:T(8,128)(2,1)S(1)}, u32[]{:S(2)}, u32[]{:S(2)}) collective-permute-start(bf16[2,128,512]{1,2,0:T(8,128)(2,1)S(1)} %get-tuple-element.144), channel_id=1, source_target_pairs={{2,0},{4,2},{6,4},{8,6},{10,8},{12,10},{14,12},{3,1},{5,3},{7,5},{... | collective-permute-start | bytes 786440 | tf_op jit(solution)/shard_map/ppermute | solution.py:20
  105.9 2.1 collective-permute-start.5
  110.3 7.6 %collective-permute-done.6 = bf16[2,128,512]{1,2,0:T(8,128)(2,1)S(1)} collective-permute-done((bf16[2,128,512]{1,2,0:T(8,128)(2,1)S(1)}, bf16[2,128,512]{1,2,0:T(8,128)(2,1)S(1)}, u32[]{:S(2)}, u32[]{:S(2)}) %collective-permute-start.6) | collective-permute-done | bytes 262176 | tf_op jit(solution)/shard_map/ppermute | solution.py:20
  120.4 3.6 %fusion.74 = (f32[8,256]{1,0:T(8,128)S(1)}, f32[8,256,256]{1,2,0:T(8,128)}) fusion(pred[256]{0:T(512)(128)(4,1)S(1)} %compare_reduce_fusion.1, bf16[256,8,64]{0,2,1:T(8,128)(2,1)} %bitcast.203, bf16[256,8,64]{0,2,1:T(8,128)(2,1)} %reshape.327), kind=kOutput, calls=%fused_computation.109 | convolution fusion | flops 69206272 | bytes 2629888 | tf_op jit(solution)/shard_map/while/body/eval_jaxpr/sub | solution.py:51
  124.0 2.8 %fusion.44 = f32[8,256,64]{1,2,0:T(8,128)} fusion(bf16[256,8,64]{0,2,1:T(8,128)(2,1)S(1)} %reshape.328, f32[8,256,256]{1,2,0:T(8,128)} %get-tuple-element.149, f32[8,256]{1,0:T(8,128)S(1)} %get-tuple-element.148), kind=kOutput, calls=%fused_computation.73 | convolution fusion | flops 68157440 | bytes 2891776 | tf_op jit(solution)/shard_map/while/body/eval_jaxpr/hqk,qhe->khe/dot_general | solution.py:67
  126.9 3.8 %fusion.30 = f32[8,256,64]{1,2,0:T(8,128)} fusion(bf16[256,8,64]{0,2,1:T(8,128)(2,1)} %reshape.327, f32[8,256,256]{2,1,0:T(8,128)S(1)} %fusion.77, f32[8,256,256]{1,2,0:T(8,128)} %get-tuple-element.149, f32[8,256]{1,0:T(8,128)S(1)} %get-tuple-element.148), kind=kOutput, calls=%fused_computation.51 | convolution fusion | flops 70781184 | bytes 4988928 | tf_op jit(solution)/shard_map/while/body/eval_jaxpr/hqk,qhe->khe/dot_general | solution.py:64
  130.6 2.3 pad_maximum_fusion.2
  133.2 9.8 %dynamic_update_slice.16 = f32[2,512,512]{1,2,0:T(8,128)S(1)} dynamic-update-slice(f32[2,512,512]{1,2,0:T(8,128)S(1)} %broadcast_in_dim.93, f32[2,256,512]{1,2,0:T(8,128)} %pad_maximum_fusion.2, s32[]{:T(128)} %constant.179.clone.1, s32[]{:T(128)S(6)} %select_n.50, s32[]{:T(128)} %constant.179.clone.1) | dynamic-update-slice | bytes 2097156 | tf_op jit(solution)/shard_map/dynamic_update_slice | solution.py:178
  146.0 3.9 %collective-permute-start.7 = (bf16[4,128,512]{1,2,0:T(8,128)(2,1)}, bf16[4,128,512]{1,2,0:T(8,128)(2,1)}, u32[]{:S(2)}, u32[]{:S(2)}) collective-permute-start(bf16[4,128,512]{1,2,0:T(8,128)(2,1)} %pad_maximum_fusion.4), channel_id=1, source_target_pairs={{2,0},{4,2},{6,4},{8,6},{10,8},{12,10},{14,12},{3,1},{5,3},{7,5},{... | collective-permute-start | bytes 1572872 | tf_op jit(solution)/shard_map/ppermute | solution.py:34
  149.9 4.9 %fusion.26 = bf16[256,8,64]{0,2,1:T(8,128)(2,1)} fusion(bf16[256,8,64]{0,2,1:T(8,128)(2,1)S(1)} %bitcast.204, f32[8,256,256]{2,1,0:T(8,128)} %copy-done.4, f32[8,256,256]{1,2,0:T(8,128)} %get-tuple-element.149, f32[8,256]{1,0:T(8,128)S(1)} %get-tuple-element.148), kind=kOutput, calls=%fused_computation.41 | convolution fusion | flops 70912256 | bytes 4726784 | tf_op jit(solution)/shard_map/while/body/eval_jaxpr/hqk,khe->qhe/dot_general | solution.py:61
  155.9 1.7 convert_element_type.83
  160.4 2.1 collective-permute-start.8
  162.5 2.7 %fusion.46 = f32[8,64,256]{2,1,0:T(8,128)} fusion(bf16[256,8,64]{0,2,1:T(8,128)(2,1)S(1)} %bitcast.189, f32[8,256,256]{1,2,0:T(8,128)} %get-tuple-element.149, f32[8,256]{1,0:T(8,128)S(1)} %get-tuple-element.148), kind=kOutput, calls=%fused_computation.75 | convolution fusion | flops 68157440 | bytes 2891776 | tf_op jit(solution)/shard_map/while/body/eval_jaxpr/hqk,khe->qhe/dot_general | solution.py:55
  167.6 10.3 %collective-permute-done.8 = bf16[4,128,512]{1,2,0:T(8,128)(2,1)S(1)} collective-permute-done((bf16[4,128,512]{1,2,0:T(8,128)(2,1)S(1)}, bf16[4,128,512]{1,2,0:T(8,128)(2,1)S(1)}, u32[]{:S(2)}, u32[]{:S(2)}) %collective-permute-start.8) | collective-permute-done | bytes 524320 | tf_op jit(solution)/shard_map/ppermute | solution.py:34
  178.0 2.2 fusion.41
  180.3 3.8 %all-to-all-start.11 = ((bf16[2,128,512]{1,2,0:T(8,128)(2,1)}), bf16[2,128,512]{1,2,0:T(8,128)(2,1)S(1)}, u32[]{:S(2)}, u32[]{:S(2)}) async-start(bf16[2,128,512]{1,2,0:T(8,128)(2,1)} %copy.101), calls=%async_computation.11 | async-start | bytes 524288 | tf_op jit(solution)/shard_map/all_to_all | solution.py:212
  184.1 2.7 %fusion.24 = bf16[256,8,64]{0,2,1:T(8,128)(2,1)S(1)} fusion(f32[8,64,256]{2,1,0:T(8,128)S(1)} %copy-done.17, bf16[512,8,64]{0,2,1:T(8,128)(2,1)S(1)} %bitcast.179, f32[8,256,512]{1,2,0:T(8,128)} %get-tuple-element.151, f32[8,256]{1,0:T(8,128)S(1)} %get-tuple-element.150), kind=kOutput, calls=%fused_computation.39 | convolution fusion | flops 136577024 | bytes 5513216 | tf_op jit(solution)/shard_map/while/body/eval_jaxpr/hqk,khe->qhe/dot_general | solution.py:55
  188.9 4.7 %all-to-all-start.6 = ((bf16[2,128,512]{1,2,0:T(8,128)(2,1)}), bf16[2,128,512]{1,2,0:T(8,128)(2,1)S(1)}, u32[]{:S(2)}, u32[]{:S(2)}) async-start(bf16[2,128,512]{1,2,0:T(8,128)(2,1)} %copy.87), calls=%async_computation.6 | async-start | bytes 524288 | tf_op jit(solution)/shard_map/all_to_all | solution.py:208
  194.5 2.6 %all-to-all-done.6 = bf16[2,128,512]{1,2,0:T(8,128)(2,1)S(1)} async-done(((bf16[2,128,512]{1,2,0:T(8,128)(2,1)}), bf16[2,128,512]{1,2,0:T(8,128)(2,1)S(1)}, u32[]{:S(2)}, u32[]{:S(2)}) %all-to-all-start.6) | async-done | bytes 262176 | tf_op jit(solution)/shard_map/all_to_all | solution.py:208
  197.1 5.2 %all-to-all-start.10 = ((bf16[2,128,512]{2,1,0:T(8,128)(2,1)}), bf16[2,128,512]{2,1,0:T(8,128)(2,1)S(1)}, u32[]{:S(2)}, u32[]{:S(2)}) async-start(bf16[2,128,512]{2,1,0:T(8,128)(2,1)} %bitcast.45), calls=%async_computation.10 | async-start | bytes 524288 | tf_op jit(solution)/shard_map/all_to_all | solution.py:211
  203.2 2.3 all-to-all-done.10
  205.5 5.4 %all-to-all-start.9 = ((bf16[2,128,512]{2,1,0:T(8,128)(2,1)}), bf16[2,128,512]{2,1,0:T(8,128)(2,1)S(1)}, u32[]{:S(2)}, u32[]{:S(2)}) async-start(bf16[2,128,512]{2,1,0:T(8,128)(2,1)} %bitcast.42), calls=%async_computation.9 | async-start | bytes 524288 | tf_op jit(solution)/shard_map/all_to_all | solution.py:210
  211.8 2.3 all-to-all-done.9
  214.1 5.4 %all-to-all-start.13 = ((bf16[2,128,512]{2,1,0:T(8,128)(2,1)}), bf16[2,128,512]{2,1,0:T(8,128)(2,1)S(1)}, u32[]{:S(2)}, u32[]{:S(2)}) async-start(bf16[2,128,512]{2,1,0:T(8,128)(2,1)} %bitcast.54), calls=%async_computation.13 | async-start | bytes 524288 | tf_op jit(solution)/shard_map/all_to_all | solution.py:214
  220.4 2.3 all-to-all-done.13
  222.7 5.4 %all-to-all-start.12 = ((bf16[2,128,512]{2,1,0:T(8,128)(2,1)}), bf16[2,128,512]{2,1,0:T(8,128)(2,1)S(1)}, u32[]{:S(2)}, u32[]{:S(2)}) async-start(bf16[2,128,512]{2,1,0:T(8,128)(2,1)} %bitcast.51), calls=%async_computation.12 | async-start | bytes 524288 | tf_op jit(solution)/shard_map/all_to_all | solution.py:213
  228.2 1.8 copy.107
  (125 shorter events, 41.2 us)
Async XLA Ops:
  0.6 14.8 %copy-start.9 = (bf16[1,128,1024]{2,1,0:T(8,128)(2,1)S(1)}, bf16[1,128,1024]{2,1,0:T(8,128)(2,1)}, u32[]{:S(2)}) copy-start(bf16[1,128,1024]{2,1,0:T(8,128)(2,1)} %param.19) | copy-start | bytes 786436
  0.6 23.4 %copy-start.10 = (bf16[1,128,1024]{2,1,0:T(8,128)(2,1)S(1)}, bf16[1,128,1024]{2,1,0:T(8,128)(2,1)}, u32[]{:S(2)}) copy-start(bf16[1,128,1024]{2,1,0:T(8,128)(2,1)} %param.20) | copy-start | bytes 786436
  2.5 22.4 %copy-start.15 = (s32[2,128]{1,0:T(2,128)S(1)}, s32[2,128]{1,0:T(2,128)}, u32[]{:S(2)}) copy-start(s32[2,128]{1,0:T(2,128)} %param.25) | copy-start | bytes 3076
  2.5 7.8 %all-to-all-start.2 = ((bf16[128,2,512]{0,2,1:T(8,128)(2,1)}), bf16[128,2,512]{0,2,1:T(8,128)(2,1)S(1)}, u32[]{:S(2)}, u32[]{:S(2)}) async-start(bf16[128,2,512]{0,2,1:T(8,128)(2,1)} %bitcast.8), calls=%async_computation.2 | async-start | bytes 524288 | tf_op jit(solution)/shard_map/all_to_all | solution.py:96
  6.6 32.0 %copy-start.16 = (s32[2,8]{1,0:T(2,128)S(1)}, s32[2,8]{1,0:T(2,128)}, u32[]{:S(2)}) copy-start(s32[2,8]{1,0:T(2,128)} %param.24) | copy-start | bytes 196
  6.6 33.9 %copy-start.11 = (bf16[1,128,1024]{2,1,0:T(8,128)(2,1)S(1)}, bf16[1,128,1024]{2,1,0:T(8,128)(2,1)}, u32[]{:S(2)}) copy-start(bf16[1,128,1024]{2,1,0:T(8,128)(2,1)} %param.21) | copy-start | bytes 786436
  8.6 32.9 %copy-start.12 = (bf16[1,128,1024]{2,1,0:T(8,128)(2,1)S(1)}, bf16[1,128,1024]{2,1,0:T(8,128)(2,1)}, u32[]{:S(2)}) copy-start(bf16[1,128,1024]{2,1,0:T(8,128)(2,1)} %param.22) | copy-start | bytes 786436
  10.3 8.3 %all-to-all-start = ((bf16[128,2,512]{2,0,1:T(8,128)(2,1)}), bf16[128,2,512]{2,0,1:T(8,128)(2,1)S(1)}, u32[]{:S(2)}, u32[]{:S(2)}) async-start(bf16[128,2,512]{2,0,1:T(8,128)(2,1)} %copy.69), calls=%async_computation | async-start | bytes 524288 | tf_op jit(solution)/shard_map/all_to_all | solution.py:97
  15.6 26.9 %copy-start.13 = (bf16[1,128,1024]{2,1,0:T(8,128)(2,1)S(1)}, bf16[1,128,1024]{2,1,0:T(8,128)(2,1)}, u32[]{:S(2)}) copy-start(bf16[1,128,1024]{2,1,0:T(8,128)(2,1)} %param.23) | copy-start | bytes 786436
  18.6 10.5 %all-to-all-start.1 = ((bf16[128,2,512]{2,0,1:T(8,128)(2,1)}), bf16[128,2,512]{2,0,1:T(8,128)(2,1)S(1)}, u32[]{:S(2)}, u32[]{:S(2)}) async-start(bf16[128,2,512]{2,0,1:T(8,128)(2,1)} %copy.71), calls=%async_computation.1 | async-start | bytes 524288 | tf_op jit(solution)/shard_map/all_to_all | solution.py:98
  29.1 14.3 %all-to-all-start.5 = ((bf16[128,2,512]{0,2,1:T(8,128)(2,1)}), bf16[128,2,512]{0,2,1:T(8,128)(2,1)S(1)}, u32[]{:S(2)}, u32[]{:S(2)}) async-start(bf16[128,2,512]{0,2,1:T(8,128)(2,1)} %bitcast.21), calls=%async_computation.5 | async-start | bytes 524288 | tf_op jit(solution)/shard_map/all_to_all | solution.py:99
  32.7 22.8 %collective-permute-start.3 = (s32[2,128]{1,0:T(2,128)S(1)}, s32[2,128]{1,0:T(2,128)S(1)}, u32[]{:S(2)}, u32[]{:S(2)}) collective-permute-start(s32[2,128]{1,0:T(2,128)S(1)} %get-tuple-element.146), channel_id=1, source_target_pairs={{2,0},{4,2},{6,4},{8,6},{10,8},{12,10},{14,12},{3,1},{5,3},{7,5},{... | collective-permute-start | bytes 3080 | tf_op jit(solution)/shard_map/ppermute | solution.py:20
  36.0 10.9 %collective-permute-start.2 = (s32[2,128]{1,0:T(2,128)S(1)}, s32[2,128]{1,0:T(2,128)S(1)}, u32[]{:S(2)}, u32[]{:S(2)}) collective-permute-start(s32[2,128]{1,0:T(2,128)S(1)} %get-tuple-element.147), channel_id=1, source_target_pairs={{0,2},{2,4},{4,6},{6,8},{8,10},{10,12},{12,14},{1,3},{3,5},{5,7},{... | collective-permute-start | bytes 3080 | tf_op jit(solution)/shard_map/ppermute | solution.py:17
  43.4 6.6 %all-to-all-start.3 = ((bf16[128,2,512]{2,0,1:T(8,128)(2,1)}), bf16[128,2,512]{2,0,1:T(8,128)(2,1)S(1)}, u32[]{:S(2)}, u32[]{:S(2)}) async-start(bf16[128,2,512]{2,0,1:T(8,128)(2,1)} %copy.78), calls=%async_computation.3 | async-start | bytes 524288 | tf_op jit(solution)/shard_map/all_to_all | solution.py:100
  50.1 12.7 %all-to-all-start.4 = ((bf16[128,2,512]{2,0,1:T(8,128)(2,1)}), bf16[128,2,512]{2,0,1:T(8,128)(2,1)S(1)}, u32[]{:S(2)}, u32[]{:S(2)}) async-start(bf16[128,2,512]{2,0,1:T(8,128)(2,1)} %copy.80), calls=%async_computation.4 | async-start | bytes 524288 | tf_op jit(solution)/shard_map/all_to_all | solution.py:101
  56.0 14.0 %collective-permute-start = (bf16[2,128,512]{1,2,0:T(8,128)(2,1)S(1)}, bf16[2,128,512]{1,2,0:T(8,128)(2,1)}, u32[]{:S(2)}, u32[]{:S(2)}) collective-permute-start(bf16[2,128,512]{1,2,0:T(8,128)(2,1)S(1)} %get-tuple-element.140), channel_id=1, source_target_pairs={{0,2},{2,4},{4,6},{6,8},{8,10},{10,12},{12,14},{1,3},{3,5},{5,7},{... | collective-permute-start | bytes 786440 | tf_op jit(solution)/shard_map/ppermute | solution.py:17
  60.3 9.7 %collective-permute-start.1 = (bf16[2,128,512]{1,2,0:T(8,128)(2,1)S(1)}, bf16[2,128,512]{1,2,0:T(8,128)(2,1)}, u32[]{:S(2)}, u32[]{:S(2)}) collective-permute-start(bf16[2,128,512]{1,2,0:T(8,128)(2,1)S(1)} %get-tuple-element.141), channel_id=1, source_target_pairs={{2,0},{4,2},{6,4},{8,6},{10,8},{12,10},{14,12},{3,1},{5,3},{7,5},{... | collective-permute-start | bytes 786440 | tf_op jit(solution)/shard_map/ppermute | solution.py:20
  62.8 6.6 %all-to-all-start.7 = ((bf16[128,2,512]{0,2,1:T(8,128)(2,1)}), bf16[128,2,512]{0,2,1:T(8,128)(2,1)S(1)}, u32[]{:S(2)}, u32[]{:S(2)}) async-start(bf16[128,2,512]{0,2,1:T(8,128)(2,1)} %bitcast.27), calls=%async_computation.7 | async-start | bytes 524288 | tf_op jit(solution)/shard_map/all_to_all | solution.py:102
  69.9 31.9 %collective-permute-start.4 = (bf16[2,256,512]{1,2,0:T(8,128)(2,1)S(1)}, bf16[2,256,512]{1,2,0:T(8,128)(2,1)S(1)}, u32[]{:S(2)}, u32[]{:S(2)}) collective-permute-start(bf16[2,256,512]{1,2,0:T(8,128)(2,1)S(1)} %pad_maximum_fusion.3), channel_id=1, source_target_pairs={{0,16},{16,0},{1,17},{17,1},{2,18},{18,2},{3,19},{19,3},{4,20},{20... | collective-permute-start | bytes 1572872 | tf_op jit(solution)/shard_map/ppermute | solution.py:28
  71.3 2.8 %copy-start.5 = (bf16[1,512,512]{1,2,0:T(8,128)(2,1)}, bf16[1,512,512]{1,2,0:T(8,128)(2,1)S(1)}, u32[]{:S(2)}) copy-start(bf16[1,512,512]{1,2,0:T(8,128)(2,1)S(1)} %get-tuple-element.135) | copy-start | bytes 1572868
  92.8 87.6 %all-to-all-start.8 = ((bf16[2,128,512]{1,2,0:T(8,128)(2,1)}), bf16[2,128,512]{1,2,0:T(8,128)(2,1)}, u32[]{:S(2)}, u32[]{:S(2)}) async-start(bf16[2,128,512]{1,2,0:T(8,128)(2,1)} %copy.91), calls=%async_computation.8 | async-start | bytes 524288 | tf_op jit(solution)/shard_map/all_to_all | solution.py:209
  101.8 7.3 %copy-start = (f32[8,512,64]{1,2,0:T(8,128)}, f32[8,512,64]{1,2,0:T(8,128)S(1)}, u32[]{:S(2)}) copy-start(f32[8,512,64]{1,2,0:T(8,128)S(1)} %fusion.32) | copy-start | bytes 3145732
  101.9 15.9 %collective-permute-start.6 = (bf16[2,128,512]{1,2,0:T(8,128)(2,1)S(1)}, bf16[2,128,512]{1,2,0:T(8,128)(2,1)S(1)}, u32[]{:S(2)}, u32[]{:S(2)}) collective-permute-start(bf16[2,128,512]{1,2,0:T(8,128)(2,1)S(1)} %get-tuple-element.144), channel_id=1, source_target_pairs={{2,0},{4,2},{6,4},{8,6},{10,8},{12,10},{14,12},{3,1},{5,3},{7,5},{... | collective-permute-start | bytes 786440 | tf_op jit(solution)/shard_map/ppermute | solution.py:20
  105.9 12.0 %collective-permute-start.5 = (bf16[2,128,512]{1,2,0:T(8,128)(2,1)S(1)}, bf16[2,128,512]{1,2,0:T(8,128)(2,1)S(1)}, u32[]{:S(2)}, u32[]{:S(2)}) collective-permute-start(bf16[2,128,512]{1,2,0:T(8,128)(2,1)S(1)} %get-tuple-element.145), channel_id=1, source_target_pairs={{0,2},{2,4},{4,6},{6,8},{8,10},{10,12},{12,14},{1,3},{3,5},{5,7},{... | collective-permute-start | bytes 786440 | tf_op jit(solution)/shard_map/ppermute | solution.py:17
  119.2 0.7 copy-start.7
  120.4 6.5 %copy-start.4 = (f32[8,256,256]{2,1,0:T(8,128)}, f32[8,256,256]{2,1,0:T(8,128)S(1)}, u32[]{:S(2)}) copy-start(f32[8,256,256]{2,1,0:T(8,128)S(1)} %fusion.77) | copy-start | bytes 6291460
  143.0 1.2 copy-start.3
  144.2 5.7 %copy-start.14 = (bf16[1,256,512]{1,2,0:T(8,128)(2,1)S(1)}, bf16[1,256,512]{1,2,0:T(8,128)(2,1)}, u32[]{:S(2)}) copy-start(bf16[1,256,512]{1,2,0:T(8,128)(2,1)} %get-tuple-element.142) | copy-start | bytes 786436
  146.0 19.2 %collective-permute-start.7 = (bf16[4,128,512]{1,2,0:T(8,128)(2,1)}, bf16[4,128,512]{1,2,0:T(8,128)(2,1)}, u32[]{:S(2)}, u32[]{:S(2)}) collective-permute-start(bf16[4,128,512]{1,2,0:T(8,128)(2,1)} %pad_maximum_fusion.4), channel_id=1, source_target_pairs={{2,0},{4,2},{6,4},{8,6},{10,8},{12,10},{14,12},{3,1},{5,3},{7,5},{... | collective-permute-start | bytes 1572872 | tf_op jit(solution)/shard_map/ppermute | solution.py:34
  154.8 7.7 %copy-start.8 = (bf16[1,256,512]{1,2,0:T(8,128)(2,1)S(1)}, bf16[1,256,512]{1,2,0:T(8,128)(2,1)}, u32[]{:S(2)}) copy-start(bf16[1,256,512]{1,2,0:T(8,128)(2,1)} %copy-done.7) | copy-start | bytes 786436
  160.4 6.1 %copy-start.2 = (f32[2,256,512]{1,2,0:T(8,128)S(1)}, f32[2,256,512]{1,2,0:T(8,128)}, u32[]{:S(2)}) copy-start(f32[2,256,512]{1,2,0:T(8,128)} %slice.231) | copy-start | bytes 3145732
  160.4 17.5 %collective-permute-start.8 = (bf16[4,128,512]{1,2,0:T(8,128)(2,1)S(1)}, bf16[4,128,512]{1,2,0:T(8,128)(2,1)S(1)}, u32[]{:S(2)}, u32[]{:S(2)}) collective-permute-start(bf16[4,128,512]{1,2,0:T(8,128)(2,1)S(1)} %pad_maximum_fusion.5), channel_id=1, source_target_pairs={{0,2},{2,4},{4,6},{6,8},{8,10},{10,12},{12,14},{1,3},{3,5},{5,7},{... | collective-permute-start | bytes 1572872 | tf_op jit(solution)/shard_map/ppermute | solution.py:34
  165.2 1.4 copy-start.1
  178.0 6.2 %copy-start.6 = (bf16[1,512,512]{1,2,0:T(8,128)(2,1)S(1)}, bf16[1,512,512]{1,2,0:T(8,128)(2,1)}, u32[]{:S(2)}) copy-start(bf16[1,512,512]{1,2,0:T(8,128)(2,1)} %copy-done.5) | copy-start | bytes 1572868
  178.0 6.1 %copy-start.17 = (f32[8,64,256]{2,1,0:T(8,128)S(1)}, f32[8,64,256]{2,1,0:T(8,128)}, u32[]{:S(2)}) copy-start(f32[8,64,256]{2,1,0:T(8,128)} %fusion.46) | copy-start | bytes 1572868
  180.3 30.7 %collective-permute-start.9 = (bf16[2,256,512]{1,2,0:T(8,128)(2,1)S(1)}, bf16[2,256,512]{1,2,0:T(8,128)(2,1)S(1)}, u32[]{:S(2)}, u32[]{:S(2)}) collective-permute-start(bf16[2,256,512]{1,2,0:T(8,128)(2,1)S(1)} %convert_element_type.84), channel_id=1, source_target_pairs={{0,16},{16,0},{1,17},{17,1},{2,18},{18,2},{3,19},{19,3},{4,20},{20... | collective-permute-start | bytes 1572872 | tf_op jit(solution)/shard_map/ppermute | solution.py:28
  180.3 8.6 %all-to-all-start.11 = ((bf16[2,128,512]{1,2,0:T(8,128)(2,1)}), bf16[2,128,512]{1,2,0:T(8,128)(2,1)S(1)}, u32[]{:S(2)}, u32[]{:S(2)}) async-start(bf16[2,128,512]{1,2,0:T(8,128)(2,1)} %copy.101), calls=%async_computation.11 | async-start | bytes 524288 | tf_op jit(solution)/shard_map/all_to_all | solution.py:212
  188.9 8.2 %all-to-all-start.6 = ((bf16[2,128,512]{1,2,0:T(8,128)(2,1)}), bf16[2,128,512]{1,2,0:T(8,128)(2,1)S(1)}, u32[]{:S(2)}, u32[]{:S(2)}) async-start(bf16[2,128,512]{1,2,0:T(8,128)(2,1)} %copy.87), calls=%async_computation.6 | async-start | bytes 524288 | tf_op jit(solution)/shard_map/all_to_all | solution.py:208
  197.1 8.3 %all-to-all-start.10 = ((bf16[2,128,512]{2,1,0:T(8,128)(2,1)}), bf16[2,128,512]{2,1,0:T(8,128)(2,1)S(1)}, u32[]{:S(2)}, u32[]{:S(2)}) async-start(bf16[2,128,512]{2,1,0:T(8,128)(2,1)} %bitcast.45), calls=%async_computation.10 | async-start | bytes 524288 | tf_op jit(solution)/shard_map/all_to_all | solution.py:211
  205.5 8.6 %all-to-all-start.9 = ((bf16[2,128,512]{2,1,0:T(8,128)(2,1)}), bf16[2,128,512]{2,1,0:T(8,128)(2,1)S(1)}, u32[]{:S(2)}, u32[]{:S(2)}) async-start(bf16[2,128,512]{2,1,0:T(8,128)(2,1)} %bitcast.42), calls=%async_computation.9 | async-start | bytes 524288 | tf_op jit(solution)/shard_map/all_to_all | solution.py:210
  214.1 8.6 %all-to-all-start.13 = ((bf16[2,128,512]{2,1,0:T(8,128)(2,1)}), bf16[2,128,512]{2,1,0:T(8,128)(2,1)S(1)}, u32[]{:S(2)}, u32[]{:S(2)}) async-start(bf16[2,128,512]{2,1,0:T(8,128)(2,1)} %bitcast.54), calls=%async_computation.13 | async-start | bytes 524288 | tf_op jit(solution)/shard_map/all_to_all | solution.py:214
  222.7 12.0 %all-to-all-start.12 = ((bf16[2,128,512]{2,1,0:T(8,128)(2,1)}), bf16[2,128,512]{2,1,0:T(8,128)(2,1)S(1)}, u32[]{:S(2)}, u32[]{:S(2)}) async-start(bf16[2,128,512]{2,1,0:T(8,128)(2,1)} %bitcast.51), calls=%async_computation.12 | async-start | bytes 524288 | tf_op jit(solution)/shard_map/all_to_all | solution.py:213
where the time goes:
time: 237 us; the launch traced here: 236 us
  starting transfers between devices  91.5 us (39%)
  matrix products  44.6 us (19%)
  local copies, waits for them, and re-layouts  42.8 us (18%)
  waiting for transfers between devices  35.5 us (15%)
  other arithmetic  14.6 us (6%)
  blocking collectives  4.23 us (2%)
  between operations  2.48 us (1%)
    unnamed x52, local copies, waits for them, and re-layouts  14.1 us
    dot_general x2, matrix products, attend(): jnp.einsum('hqk,khe->qhe', grad_scores, k_heads, preferred_element_type=j...  12.2 us
    dot_general x2, matrix products, attend(): jnp.einsum('hqk,qhe->khe', grad_scores, q_heads, preferred_element_type=j...  10.9 us
    ppermute x2, waiting for transfers between devices, passed_along(): return lax.ppermute(block, axis, route)  10.3 us
    dynamic_update_slice x1, local copies, waits for them, and re-layouts, shards(): lax.dynamic_update_slice_in_dim(cross_ext, jnp.stack((cross_gk, cross_gv)...  9.82 us
    ppermute x3, starting transfers between devices, extended(): lax.ppermute(lax.slice_in_dim(block, 0, width, axis=dim), axis, backward)  9.67 us
    ppermute x3, starting transfers between devices, extended(): lax.ppermute(lax.slice_in_dim(block, block.shape[dim] - width, None, axis...  8.96 us
    ppermute x3, waiting for transfers between devices, extended(): lax.ppermute(lax.slice_in_dim(block, 0, width, axis=dim), axis, backward)  7.58 us
  transfers between devices with their start and end apart: 24, of which 10 were waited for; matrix products, arithmetic and copies ran while one was open for 41% of the time, Pallas kernels for 0%

commit v1 on v0

--- a/solution.py
+++ b/solution.py
@@ -1,12 +1,452 @@
+import functools
+
 import jax
 import jax.numpy as jnp
 from jax import lax
+from jax.experimental import pallas as pl
+from jax.experimental.pallas import tpu as pltpu
 from jax.sharding import PartitionSpec as P
 
 HEADS = 16
 HEAD = 64
 WINDOW = 2048
 TILE = 512
+MESH = pl.DeviceIdType.MESH
+F32, BF16 = jnp.float32, jnp.bfloat16
+
+
+def places():
+    tower, blk, seq = lax.axis_index("tower"), lax.axis_index("blk"), lax.axis_index("seq")
+    peers = dict(
+        y=(tower, blk, 1 - seq),
+        tower=(1 - tower, blk, seq),
+        diag=(1 - tower, blk, 1 - seq),
+        low=(tower, blk - 1, seq),
+        high=(tower, blk + 1, seq),
+    )
+    return tower, blk, seq, peers
+
+
+def greet(blk, blks, peers):
+    barrier = pltpu.get_barrier_semaphore()
+    for name in ("y", "tower", "diag"):
+        pl.semaphore_signal(barrier, inc=1, device_id=peers[name], device_id_type=MESH)
+
+    @pl.when(blk > 0)
+    def _():
+        pl.semaphore_signal(barrier, inc=1, device_id=peers["low"], device_id_type=MESH)
+
+    @pl.when(blk < blks - 1)
+    def _():
+        pl.semaphore_signal(barrier, inc=1, device_id=peers["high"], device_id_type=MESH)
+
+    count = 3 + jnp.where(blk > 0, 1, 0) + jnp.where(blk < blks - 1, 1, 0)
+    pl.semaphore_wait(barrier, count)
+
+
+def remote(src, dst, send, recv, device):
+    return pltpu.make_async_remote_copy(
+        src_ref=src, dst_ref=dst, send_sem=send, recv_sem=recv,
+        device_id=device, device_id_type=MESH,
+    )
+
+
+def gather_kernel(
+    blks, cols, q_ref, k_ref, v_ref, cq_ref, ck_ref, cv_ref, g_ref, m_ref,
+    yk, yv, yq, yg, ycq, part_own, part_y, ymask, low_halo, high_halo, low_mask, high_mask,
+    send_sem, recv_sem, low_send, low_recv, high_send, high_recv,
+):
+    tower, blk, seq, peers = places()
+    greet(blk, blks, peers)
+    mine = pl.ds(pl.multiple_of(seq * cols, cols), cols)
+    theirs = pl.ds(pl.multiple_of((1 - seq) * cols, cols), cols)
+    first = [
+        remote(m_ref, ymask, send_sem.at[0], recv_sem.at[0], peers["y"]),
+        remote(k_ref.at[:, theirs], yk, send_sem.at[1], recv_sem.at[1], peers["y"]),
+        remote(v_ref.at[:, theirs], yv, send_sem.at[2], recv_sem.at[2], peers["y"]),
+        remote(ck_ref.at[:, theirs], part_y.at[0], send_sem.at[3], recv_sem.at[3], peers["diag"]),
+        remote(cv_ref.at[:, theirs], part_y.at[1], send_sem.at[4], recv_sem.at[4], peers["diag"]),
+        remote(ck_ref.at[:, mine], part_own.at[0], send_sem.at[5], recv_sem.at[5], peers["tower"]),
+        remote(cv_ref.at[:, mine], part_own.at[1], send_sem.at[6], recv_sem.at[6], peers["tower"]),
+        remote(q_ref.at[:, theirs], yq, send_sem.at[7], recv_sem.at[7], peers["y"]),
+        remote(g_ref.at[:, theirs], yg, send_sem.at[8], recv_sem.at[8], peers["y"]),
+        remote(cq_ref.at[:, theirs], ycq, send_sem.at[9], recv_sem.at[9], peers["y"]),
+    ]
+    own_sources = [k_ref.at[:, mine], v_ref.at[:, mine], part_own.at[0], part_own.at[1], m_ref]
+    far_sources = [yk, yv, part_y.at[0], part_y.at[1], ymask]
+    own_waits = [None, None, first[5], first[6], None]
+    far_waits = [first[1], first[2], first[3], first[4], first[0]]
+
+    def up(sources, at):
+        target = high_dst[at]
+        return remote(sources[at], target, high_send.at[at], high_recv.at[at], peers["high"])
+
+    def down(sources, at):
+        target = low_dst[at]
+        return remote(sources[at], target, low_send.at[at], low_recv.at[at], peers["low"])
+
+    high_dst = [low_halo.at[0], low_halo.at[1], low_halo.at[2], low_halo.at[3], low_mask]
+    low_dst = [high_halo.at[0], high_halo.at[1], high_halo.at[2], high_halo.at[3], high_mask]
+    has_low, has_high = blk > 0, blk < blks - 1
+    for copy in first[:5]:
+        copy.start()
+    first[5].start()
+    first[6].start()
+    order = (4, 0, 1, 2, 3)
+    own_high, own_low = seq == 1, seq == 0
+    for copy in first[7:]:
+        copy.start()
+
+    def pass_on(sources, waits, pick_high, pick_low):
+        for at in order:
+            if waits[at] is not None:
+                waits[at].wait_recv()
+
+            @pl.when(pick_high & has_high)
+            def _():
+                up(sources, at).start()
+
+            @pl.when(pick_low & has_low)
+            def _():
+                down(sources, at).start()
+
+    pass_on(own_sources, own_waits, own_high, own_low)
+    pass_on(far_sources, far_waits, own_low, own_high)
+    for copy in first[7:]:
+        copy.wait_recv()
+    for copy in first:
+        copy.wait_send()
+
+    @pl.when(has_high)
+    def _():
+        for at in order:
+            up(far_sources, at).wait_send()
+            down(far_sources, at).wait_recv()
+
+    @pl.when(has_low)
+    def _():
+        for at in order:
+            down(far_sources, at).wait_send()
+            up(far_sources, at).wait_recv()
+
+
+def attend_kernel(
+    blks, rows, cols,
+    off_ref, q_ref, k_ref, v_ref, cq_ref, g_ref, m_ref,
+    yk, yv, yq, yg, ycq, part_own, part_y, ymask, low_halo, high_halo, low_mask, high_mask,
+    y_out, own_out, low_out, high_out, core_out,
+    q_s, g_s, cq_s, ext, ext_t, bias, head_t,
+):
+    tower, blk, seq, _ = places()
+    half = rows
+    keys = 3 * half
+    scale = HEAD ** (-0.5)
+    here = pl.ds(pl.multiple_of(seq * half, half), half)
+    there = pl.ds(pl.multiple_of((1 - seq) * half, half), half)
+    mine = pl.ds(pl.multiple_of(seq * cols, cols), cols)
+    ext_here = pl.ds(pl.multiple_of((1 + seq) * half, half), half)
+    ext_there = pl.ds(pl.multiple_of((2 - seq) * half, half), half)
+    q_s[here, :] = q_ref[:, mine] * BF16(scale)
+    q_s[there, :] = yq[...] * BF16(scale)
+    cq_s[here, :] = cq_ref[:, mine] * BF16(scale)
+    cq_s[there, :] = ycq[...] * BF16(scale)
+    g_s[here, :] = g_ref[:, mine]
+    g_s[there, :] = yg[...]
+    own_sides = [k_ref[:, mine], v_ref[:, mine], part_own[0], part_own[1]]
+    far_sides = [yk[...], yv[...], part_y[0], part_y[1]]
+    for at in range(4):
+        ext[at, ext_here, :] = own_sides[at]
+        ext[at, ext_there, :] = far_sides[at]
+        ext[at, :half, :] = jnp.where(blk > 0, low_halo[at], jnp.zeros_like(low_halo[at]))
+        ext[at, 3 * half :, :] = jnp.where(
+            blk < blks - 1, high_halo[at], jnp.zeros_like(high_halo[at])
+        )
+    for at in range(4):
+        ext_t[at] = jnp.transpose(ext[at].astype(F32)).astype(BF16)
+
+    off = off_ref[tower, blk]
+    cross_at = pl.multiple_of(jnp.where(off < 0, 0, half), half)
+    band_low = off + half
+
+    def column(row):
+        wide = jnp.broadcast_to(row.astype(F32), (half, half))
+        return jnp.transpose(wide)
+
+    low_ok = jnp.where(blk > 0, 1, 0)
+    high_ok = jnp.where(blk < blks - 1, 1, 0)
+
+    def valid_parts(chain):
+        at = pl.ds(chain, 1)
+        own, far = m_ref[at, :], ymask[at, :]
+        first = jnp.where(seq == 0, own, far)
+        second = jnp.where(seq == 0, far, own)
+        low = jnp.where(low_ok > 0, low_mask[at, :], 0)
+        high = jnp.where(high_ok > 0, high_mask[at, :], 0)
+        return [column(low), column(first), column(second), column(high)]
+
+    own_valid = valid_parts(tower)
+    other_valid = valid_parts(1 - tower)
+    row_at = lax.broadcasted_iota(jnp.int32, (half, half), 0)
+    col_at = lax.broadcasted_iota(jnp.int32, (half, half), 1)
+    for tile in range(2):
+        for part in range(3):
+            distance = col_at + half - (row_at + part * half)
+            near = (jnp.abs(distance) <= half) & (own_valid[tile + part] > 0)
+            add = jnp.where(near, 0.0, -1e30)
+            bias[tile, part * half : (part + 1) * half, :half] = add
+            bias[tile, part * half : (part + 1) * half, half:] = add
+    for part in range(3):
+        at = row_at + part * half + cross_at
+        valid = jnp.where(off < 0, other_valid[part], other_valid[part + 1])
+        inside = (at >= band_low) & (at < band_low + 2 * half) & (valid > 0)
+        add = jnp.where(inside, 0.0, -1e30)
+        bias[2, part * half : (part + 1) * half, :half] = add
+        bias[2, part * half : (part + 1) * half, half:] = add
+
+    wide = 2 * HEAD
+    lanes = lax.broadcasted_iota(jnp.int32, (half, wide), 1)
+    zero = jnp.zeros((half, wide), BF16)
+
+    def split(tile):
+        return jnp.concatenate(
+            (jnp.where(lanes < HEAD, tile, zero), jnp.where(lanes < HEAD, zero, tile)), 0
+        )
+
+    def dot_t(a, b):
+        return lax.dot_general(a, b, (((1,), (1,)), ((), ())), preferred_element_type=F32)
+
+    def dot(a, b):
+        return jnp.dot(a, b, preferred_element_type=F32)
+
+    def own_heads(both):
+        return jnp.concatenate((both[:HEAD, :half], both[HEAD:, half:]), 0)
+
+    def one(pair, query, cot, which, start, add):
+        at = pl.ds(pl.multiple_of(pair * wide, wide), wide)
+        span = pl.ds(start, keys)
+        key = ext[which, span, at]
+        value = ext[which + 1, span, at]
+        key_t = ext_t[which, at, span]
+        value_t = ext_t[which + 1, at, span]
+        scores = dot_t(key, query) + bias[add]
+        unnormed = jnp.exp(scores - jnp.max(scores, axis=0, keepdims=True))
+        weights = unnormed * (1.0 / jnp.sum(unnormed, axis=0, keepdims=True))
+        prob = weights.astype(BF16)
+        grad_probs = dot_t(value, cot)
+        row_dot = jnp.sum(weights * grad_probs, axis=0, keepdims=True)
+        grad_scores = (weights * (grad_probs - row_dot)).astype(BF16)
+        result = own_heads(dot(value_t, prob))
+        grad_query = own_heads(dot(key_t, grad_scores)) * scale
+        return result, grad_query, dot(grad_scores, query), dot(prob, cot)
+
+    zero_half = jnp.zeros((half, wide), F32)
+
+    def pair_step(pair, carry):
+        at = pl.ds(pl.multiple_of(pair * wide, wide), wide)
+        outs = []
+        for tile in range(2):
+            tile_rows = slice(tile * half, (tile + 1) * half)
+            cot = split(g_s[tile_rows, at])
+            query = split(q_s[tile_rows, at])
+            cross = split(cq_s[tile_rows, at])
+            mine_o, mine_q, mine_k, mine_v = one(pair, query, cot, 0, tile * half, tile)
+            other_o, other_q, other_k, other_v = one(pair, cross, cot, 2, cross_at, 2)
+            head_t[0, at, tile_rows] = mine_o + other_o
+            head_t[1, at, tile_rows] = mine_q
+            head_t[2, at, tile_rows] = other_q
+            outs.append((mine_k, mine_v, other_k, other_v))
+        for slot in range(2):
+            first, second = outs[0][slot], outs[1][slot]
+            low_out[slot, :, at] = first[:half].astype(BF16)
+            core_out[slot, 0, :, at] = first[half : 2 * half] + second[:half]
+            core_out[slot, 1, :, at] = first[2 * half :] + second[half : 2 * half]
+            high_out[slot, :, at] = second[2 * half :].astype(BF16)
+        below = off < 0
+        for slot in range(2, 4):
+            total = outs[0][slot] + outs[1][slot]
+            a, b, c = total[:half], total[half : 2 * half], total[2 * half :]
+            low_out[slot, :, at] = jnp.where(below, a, zero_half).astype(BF16)
+            core_out[slot, 0, :, at] = jnp.where(below, b, a)
+            core_out[slot, 1, :, at] = jnp.where(below, c, b)
+            high_out[slot, :, at] = jnp.where(below, zero_half, c).astype(BF16)
+        return carry
+
+    lax.fori_loop(0, cols // wide, pair_step, 0)
+    for slot in range(3):
+        whole = jnp.transpose(head_t[slot]).astype(BF16)
+        lower, upper = whole[:half], whole[half:]
+        own_out[slot] = jnp.where(seq == 0, lower, upper)
+        y_out[slot] = jnp.where(seq == 0, upper, lower)
+
+
+def scatter_kernel(
+    blks, cols, y_in, own_in, low_in, high_in, core_in,
+    o_out, gq_out, gk_out, gv_out, gcq_out, gck_out, gcv_out,
+    recv, y_send, tower_send,
+    a_send, a_recv, low_send, low_recv, high_send, high_recv,
+):
+    tower, blk, seq, peers = places()
+    greet(blk, blks, peers)
+    mine = pl.ds(pl.multiple_of(seq * cols, cols), cols)
+    has_low, has_high = blk > 0, blk < blks - 1
+    direct = [o_out, gq_out, gcq_out]
+    grads = [gk_out, gv_out, gck_out, gcv_out]
+
+    def down(at):
+        return remote(low_in.at[at], recv.at[1, at], low_send.at[at], low_recv.at[at], peers["low"])
+
+    def up(at):
+        return remote(high_in.at[at], recv.at[0, at], high_send.at[at], high_recv.at[at], peers["high"])
+
+    def start_down():
+        @pl.when(has_low)
+        def _():
+            for at in range(4):
+                down(at).start()
+
+    def start_up():
+        @pl.when(has_high)
+        def _():
+            for at in range(4):
+                up(at).start()
+
+    @pl.when(seq == 0)
+    def _():
+        start_down()
+        start_up()
+
+    @pl.when(seq == 1)
+    def _():
+        start_up()
+        start_down()
+
+    sent = [
+        remote(y_in.at[at], direct[at].at[:, mine], a_send.at[at], a_recv.at[at], peers["y"])
+        for at in range(3)
+    ]
+    for copy in sent:
+        copy.start()
+    for at in range(3):
+        direct[at][:, mine] = own_in[at]
+
+    @pl.when(blk == 0)
+    def _():
+        recv[0] = jnp.zeros(recv.shape[1:], BF16)
+
+    @pl.when(blk == blks - 1)
+    def _():
+        recv[1] = jnp.zeros(recv.shape[1:], BF16)
+
+    def take(low_side, high_side, at):
+        @pl.when(low_side & has_low)
+        def _():
+            up(at).wait_recv()
+
+        @pl.when(high_side & has_high)
+        def _():
+            down(at).wait_recv()
+
+    for at in range(4):
+        take(seq == 1, seq == 0, at)
+        y_send[at] = (core_in[at, 1 - seq] + recv[1 - seq, at].astype(F32)).astype(BF16)
+        copy = remote(
+            y_send.at[at], grads[at].at[:, mine], a_send.at[3 + at], a_recv.at[3 + at],
+            peers["y" if at < 2 else "diag"],
+        )
+        copy.start()
+        sent.append(copy)
+    for at in (2, 3, 0, 1):
+        take(seq == 0, seq == 1, at)
+        total = (core_in[at, seq] + recv[seq, at].astype(F32)).astype(BF16)
+        if at < 2:
+            grads[at][:, mine] = total
+        else:
+            tower_send[at - 2] = total
+            copy = remote(
+                tower_send.at[at - 2], grads[at].at[:, mine], a_send.at[5 + at], a_recv.at[5 + at],
+                peers["tower"],
+            )
+            copy.start()
+            sent.append(copy)
+    for copy in sent:
+        copy.wait()
+
+    @pl.when(has_low)
+    def _():
+        for at in range(4):
+            down(at).wait_send()
+
+    @pl.when(has_high)
+    def _():
+        for at in range(4):
+            up(at).wait_send()
+
+
+def paired(
+    queries, key_rows, value_rows, cross_queries, cross_keys, cross_values, grad_out,
+    offsets, key_valid,
+):
+    blks = lax.axis_size("blk")
+    heads_here = HEADS // lax.axis_size("seq")
+    cols = heads_here * HEAD
+    q, k, v, cq, ck, cv, g = (
+        value[0] for value in (
+            queries, key_rows, value_rows, cross_queries, cross_keys, cross_values, grad_out
+        )
+    )
+    rows = q.shape[0]
+    block = 2 * rows
+    any_spec = pl.BlockSpec(memory_space=pl.ANY)
+    vmem = pl.BlockSpec(memory_space=pltpu.VMEM)
+    shape = jax.ShapeDtypeStruct
+    side = shape((rows, cols), BF16)
+    mask = shape(key_valid.shape, key_valid.dtype)
+    dma = pltpu.SemaphoreType.DMA
+    gathered = pl.pallas_call(
+        functools.partial(gather_kernel, blks, cols),
+        out_shape=(
+            side, side, side, side, side,
+            shape((2, rows, cols), BF16), shape((2, rows, cols), BF16), mask,
+            shape((4, rows, cols), BF16), shape((4, rows, cols), BF16), mask, mask,
+        ),
+        in_specs=[any_spec] * 8,
+        out_specs=(any_spec,) * 12,
+        scratch_shapes=[dma((10,)), dma((10,)), dma((5,)), dma((5,)), dma((5,)), dma((5,))],
+        compiler_params=pltpu.CompilerParams(collective_id=0, has_side_effects=True),
+        name="gather_in",
+    )(q, k, v, cq, ck, cv, g, key_valid)
+    results = pl.pallas_call(
+        functools.partial(attend_kernel, blks, rows, cols),
+        out_shape=(
+            shape((3, rows, cols), BF16), shape((3, rows, cols), BF16),
+            shape((4, rows, cols), BF16), shape((4, rows, cols), BF16),
+            shape((4, 2, rows, cols), F32),
+        ),
+        in_specs=[pl.BlockSpec(memory_space=pltpu.SMEM)] + [vmem] * 18,
+        out_specs=(vmem,) * 5,
+        scratch_shapes=[
+            pltpu.VMEM((block, cols), BF16), pltpu.VMEM((block, cols), BF16),
+            pltpu.VMEM((block, cols), BF16),
+            pltpu.VMEM((4, 2 * block, cols), BF16), pltpu.VMEM((4, cols, 2 * block), BF16),
+            pltpu.VMEM((3, 3 * rows, block), F32), pltpu.VMEM((3, cols, block), F32),
+        ],
+        name="attend",
+    )(offsets, q, k, v, cq, g, key_valid, *gathered)
+    full = shape((rows, 2 * cols), BF16)
+    outs = pl.pallas_call(
+        functools.partial(scatter_kernel, blks, cols),
+        out_shape=(full,) * 7,
+        in_specs=[vmem] * 5,
+        out_specs=(vmem,) * 7,
+        scratch_shapes=[
+            pltpu.VMEM((2, 4, rows, cols), BF16), pltpu.VMEM((4, rows, cols), BF16),
+            pltpu.VMEM((2, rows, cols), BF16),
+            dma((9,)), dma((9,)), dma((4,)), dma((4,)), dma((4,)), dma((4,)),
+        ],
+        compiler_params=pltpu.CompilerParams(collective_id=1, has_side_effects=True),
+        name="scatter_out",
+    )(*results)
+    return tuple(piece[None] for piece in outs)
 
 
 def extended(block, sides, width):
@@ -237,4 +677,5 @@
         P("tower", ("blk", "seq"), None),
         P("tower", ("blk", "seq"), None),
     )
-    return jax.shard_map(shards, mesh=mesh, in_specs=in_specs, out_specs=out_specs, check_vma=False)
+    body = paired if mesh.shape["seq"] == 2 else shards
+    return jax.shard_map(body, mesh=mesh, in_specs=in_specs, out_specs=out_specs, check_vma=False)

time: 237 us -> 85 us (0.36)
  the two profiles are of different devices: /device:TPU:12 before, /device:TPU:17 now
where the time goes in v1:
time: 85 us; the launch traced here: 83.4 us
  Pallas kernels  73.9 us (87%)
  local copies, waits for them, and re-layouts  8.86 us (10%)
    pallas_call x1, Pallas kernels, paired(): pl.pallas_call(functools.partial(scatter_kernel, blks, cols), out_shape=(...  32.4 us
    pallas_call x1, Pallas kernels, paired(): pl.pallas_call(functools.partial(gather_kernel, blks, cols), out_shape=(s...  26.9 us
    pallas_call x1, Pallas kernels, paired(): pl.pallas_call(functools.partial(attend_kernel, blks, rows, cols), out_sh...  14.5 us
    unnamed x13, local copies, waits for them, and re-layouts  8.86 us

profile of v1, /device:TPU:17, one launch (start us, length us, event | category | flops | bytes accessed | tf_op | source)
XLA Modules:
  0.0 83.4 jit_solution(4348420530338873771)
XLA Ops:
  0.6 26.9 %gather_in.1 = (bf16[128,512]{1,0:T(8,128)(2,1)}, bf16[128,512]{1,0:T(8,128)(2,1)}, bf16[128,512]{1,0:T(8,128)(2,1)}, bf16[128,512]{1,0:T(8,128)(2,1)}, bf16[128...) custom-call(bf16[128,1024]{1,0:T(8,128)(2,1)} %bitcast.14, ...), custom_call_target="tpu_custom_call" | custom-call | tf_op jit(solution)/shard_map/gather_in/pallas_call | solution.py:405
  27.6 14.5 %attend.1 = (bf16[3,128,512]{2,1,0:T(8,128)(2,1)}, bf16[3,128,512]{2,1,0:T(8,128)(2,1)}, bf16[4,128,512]{2,1,0:T(8,128)(2,1)}, bf16[4,128,512]{2,1,0:T(8,128)(2,1)}, f32[4,2,128,512]{3,2,1,0:T(8,128)}) custom-call(s32[2,8]{1,0:T(2,128)} %off_ref.1, bf16[128,1024]{1,0:T(8,128)(2,1)} %bitcast.15, bf16[128,1024]{1,0:T(8,128)(2,1)} %bitcast.17, ...), custom_call_target="tpu_custom_call" | custom-call | tf_op jit(solution)/shard_map/attend/pallas_call | solution.py:418
  42.1 32.4 %scatter_out.1 = (bf16[128,1024]{1,0:T(8,128)(2,1)}, bf16[128,1024]{1,0:T(8,128)(2,1)}, bf16[128,1024]{1,0:T(8,128)(2,1)}, bf16[128,1024]{1,0:T(8,128)(2,1)}, bf...) custom-call(bf16[3,128,512]{2,1,0:T(8,128)(2,1)} %get-tuple-element.43.y_in, ...), custom_call_target="tpu_custom_call" | custom-call | tf_op jit(solution)/shard_map/scatter_out/pallas_call | solution.py:436
  74.5 0.0 copy-start.2
  74.5 0.0 copy-start.1
  74.5 0.0 copy-start
  74.6 1.7 %copy.23 = bf16[1,128,1024]{2,1,0:T(8,128)(2,1)} copy(bf16[1,128,1024]{2,1,0:T(8,128)(2,1)} %bitcast.32) | data formatting | bytes 524288
  76.3 1.7 %copy.24 = bf16[1,128,1024]{2,1,0:T(8,128)(2,1)} copy(bf16[1,128,1024]{2,1,0:T(8,128)(2,1)} %bitcast.31) | data formatting | bytes 524288
  78.0 1.7 %copy.25 = bf16[1,128,1024]{2,1,0:T(8,128)(2,1)} copy(bf16[1,128,1024]{2,1,0:T(8,128)(2,1)} %bitcast.30) | data formatting | bytes 524288
  79.6 1.7 %copy.26 = bf16[1,128,1024]{2,1,0:T(8,128)(2,1)} copy(bf16[1,128,1024]{2,1,0:T(8,128)(2,1)} %bitcast.29) | data formatting | bytes 524288
  81.3 0.0 copy-done.2
  81.3 0.7 copy.27
  82.0 0.0 copy-done.1
  82.0 0.7 copy.28
  82.7 0.0 copy-done
  82.7 0.7 copy.29
Async XLA Ops:
  74.5 6.8 %copy-start.2 = (bf16[128,1024]{1,0:T(8,128)(2,1)S(1)}, bf16[128,1024]{1,0:T(8,128)(2,1)}, u32[]{:S(2)}) copy-start(bf16[128,1024]{1,0:T(8,128)(2,1)} %get-tuple-element.52) | copy-start | bytes 786436
  74.5 7.5 %copy-start.1 = (bf16[128,1024]{1,0:T(8,128)(2,1)S(1)}, bf16[128,1024]{1,0:T(8,128)(2,1)}, u32[]{:S(2)}) copy-start(bf16[128,1024]{1,0:T(8,128)(2,1)} %get-tuple-element.53) | copy-start | bytes 786436
  74.5 8.2 %copy-start = (bf16[128,1024]{1,0:T(8,128)(2,1)S(1)}, bf16[128,1024]{1,0:T(8,128)(2,1)}, u32[]{:S(2)}) copy-start(bf16[128,1024]{1,0:T(8,128)(2,1)} %get-tuple-element.54) | copy-start | bytes 786436

commit v2 on v0

--- a/solution.py
+++ b/solution.py
@@ -1,12 +1,496 @@
+import functools
+
 import jax
 import jax.numpy as jnp
 from jax import lax
+from jax.experimental import pallas as pl
+from jax.experimental.pallas import tpu as pltpu
 from jax.sharding import PartitionSpec as P
 
 HEADS = 16
 HEAD = 64
 WINDOW = 2048
 TILE = 512
+MESH = pl.DeviceIdType.MESH
+F32, BF16 = jnp.float32, jnp.bfloat16
+
+
+def places():
+    tower, blk, seq = lax.axis_index("tower"), lax.axis_index("blk"), lax.axis_index("seq")
+    peers = dict(
+        y=(tower, blk, 1 - seq),
+        tower=(1 - tower, blk, seq),
+        diag=(1 - tower, blk, 1 - seq),
+        low=(tower, blk - 1, seq),
+        high=(tower, blk + 1, seq),
+    )
+    return tower, blk, seq, peers
+
+
+def greet(blk, blks, peers):
+    barrier = pltpu.get_barrier_semaphore()
+    for name in ("y", "tower", "diag"):
+        pl.semaphore_signal(barrier, inc=1, device_id=peers[name], device_id_type=MESH)
+
+    @pl.when(blk > 0)
+    def _():
+        pl.semaphore_signal(barrier, inc=1, device_id=peers["low"], device_id_type=MESH)
+
+    @pl.when(blk < blks - 1)
+    def _():
+        pl.semaphore_signal(barrier, inc=1, device_id=peers["high"], device_id_type=MESH)
+
+    count = 3 + jnp.where(blk > 0, 1, 0) + jnp.where(blk < blks - 1, 1, 0)
+    pl.semaphore_wait(barrier, count)
+
+
+def remote(src, dst, send, recv, device):
+    return pltpu.make_async_remote_copy(
+        src_ref=src, dst_ref=dst, send_sem=send, recv_sem=recv,
+        device_id=device, device_id_type=MESH,
+    )
+
+
+def fused_kernel(
+    blks, rows, cols,
+    off_ref, q_ref, k_ref, v_ref, cq_ref, ck_ref, cv_ref, g_ref, m_ref,
+    o_out, gq_out, gk_out, gv_out, gcq_out, gck_out, gcv_out,
+    side, ext, mask_ext, bias, y_stage, t_stage, low_stage, high_stage, core, recv,
+    local_sem, mask_send, mask_recv, in_send, in_recv,
+    low_send, low_recv, high_send, high_recv,
+    out_send, out_recv, glow_send, glow_recv, ghigh_send, ghigh_recv,
+):
+    tower, blk, seq, peers = places()
+    half, wide = rows, 2 * HEAD
+    keys, groups = 3 * rows, cols // (2 * HEAD)
+    scale = HEAD ** (-0.5)
+    has_low, has_high = blk > 0, blk < blks - 1
+    here = pl.ds(pl.multiple_of(seq * half, half), half)
+    ext_here = pl.ds(pl.multiple_of((1 + seq) * half, half), half)
+    mine = pl.ds(pl.multiple_of(seq * cols, cols), cols)
+    inner_low, inner_high = pl.ds(half, half), pl.ds(2 * half, half)
+    outer_low, outer_high = pl.ds(0, half), pl.ds(3 * half, half)
+    direct = [o_out, gq_out, gcq_out]
+    grads = [gk_out, gv_out, gck_out, gcv_out]
+
+    def strip(g, base=0):
+        return pl.ds(pl.multiple_of(base + g * wide, wide), wide)
+
+    def incoming(g):
+        at = strip(g)
+        keep, give = strip(g, seq * cols), strip(g, (1 - seq) * cols)
+        moves = [
+            (k_ref.at[:, give], ext.at[0, ext_here, at], "y"),
+            (v_ref.at[:, give], ext.at[1, ext_here, at], "y"),
+            (ck_ref.at[:, give], ext.at[2, ext_here, at], "diag"),
+            (cv_ref.at[:, give], ext.at[3, ext_here, at], "diag"),
+            (ck_ref.at[:, keep], ext.at[2, ext_here, at], "tower"),
+            (cv_ref.at[:, keep], ext.at[3, ext_here, at], "tower"),
+            (q_ref.at[:, give], side.at[0, here, at], "y"),
+            (g_ref.at[:, give], side.at[2, here, at], "y"),
+            (cq_ref.at[:, give], side.at[1, here, at], "y"),
+        ]
+        return [
+            remote(src, dst, in_send.at[g, i], in_recv.at[g, i], peers[to])
+            for i, (src, dst, to) in enumerate(moves)
+        ]
+
+    def up(g, i):
+        at = strip(g)
+        return remote(
+            ext.at[i, inner_high, at], ext.at[i, outer_low, at],
+            high_send.at[g, i], high_recv.at[g, i], peers["high"],
+        )
+
+    def down(g, i):
+        at = strip(g)
+        return remote(
+            ext.at[i, inner_low, at], ext.at[i, outer_high, at],
+            low_send.at[g, i], low_recv.at[g, i], peers["low"],
+        )
+
+    mask_y = remote(m_ref, mask_ext.at[1 + seq], mask_send.at[0], mask_recv.at[0], peers["y"])
+    mask_up = remote(mask_ext.at[2], mask_ext.at[0], mask_send.at[1], mask_recv.at[1], peers["high"])
+    mask_down = remote(mask_ext.at[1], mask_ext.at[3], mask_send.at[2], mask_recv.at[2], peers["low"])
+
+    def pass_on(g, own):
+        moved = incoming(g)
+        to_high = (seq == 1) if own else (seq == 0)
+        to_low = (seq == 0) if own else (seq == 1)
+        for i in range(4):
+            if not own:
+                moved[i].wait_recv()
+            elif i >= 2:
+                moved[i + 2].wait_recv()
+
+            @pl.when(to_high & has_high)
+            def _():
+                up(g, i).start()
+
+            @pl.when(to_low & has_low)
+            def _():
+                down(g, i).start()
+
+    locals_ = [
+        pltpu.make_async_copy(k_ref.at[:, mine], ext.at[0, ext_here, :], local_sem.at[0]),
+        pltpu.make_async_copy(v_ref.at[:, mine], ext.at[1, ext_here, :], local_sem.at[1]),
+        pltpu.make_async_copy(m_ref, mask_ext.at[1 + seq], local_sem.at[2]),
+        pltpu.make_async_copy(q_ref.at[:, mine], side.at[0, here, :], local_sem.at[3]),
+        pltpu.make_async_copy(cq_ref.at[:, mine], side.at[1, here, :], local_sem.at[4]),
+        pltpu.make_async_copy(g_ref.at[:, mine], side.at[2, here, :], local_sem.at[5]),
+    ]
+    for copy in locals_:
+        copy.start()
+
+    @pl.when(blk == 0)
+    def _():
+        ext[:, :half, :] = jnp.zeros((4, half, cols), BF16)
+        mask_ext[0] = jnp.zeros(mask_ext.shape[1:], jnp.int32)
+        recv[0] = jnp.zeros(recv.shape[1:], BF16)
+
+    @pl.when(blk == blks - 1)
+    def _():
+        ext[:, 3 * half :, :] = jnp.zeros((4, half, cols), BF16)
+        mask_ext[3] = jnp.zeros(mask_ext.shape[1:], jnp.int32)
+        recv[1] = jnp.zeros(recv.shape[1:], BF16)
+
+    greet(blk, blks, peers)
+    mask_y.start()
+    for g in range(groups + 1):
+        if g < groups:
+            for copy in incoming(g)[:6]:
+                copy.start()
+        if g > 0:
+            for copy in incoming(g - 1)[6:]:
+                copy.start()
+    for copy in locals_:
+        copy.wait()
+    pass_on(0, True)
+    mask_y.wait_recv()
+
+    @pl.when(has_high)
+    def _():
+        mask_up.start()
+
+    @pl.when(has_low)
+    def _():
+        mask_down.start()
+
+    pass_on(0, False)
+    if groups > 1:
+        pass_on(1, True)
+
+    @pl.when(has_high)
+    def _():
+        mask_down.wait_recv()
+
+    @pl.when(has_low)
+    def _():
+        mask_up.wait_recv()
+
+    off = off_ref[tower, blk]
+    below = off < 0
+    cross_at = jnp.where(below, 0, half)
+    band_low = off + half
+
+    def column(part, chain):
+        row = jnp.where(
+            chain == 0, mask_ext[part, 0:1, :].astype(F32), mask_ext[part, 1:2, :].astype(F32)
+        )
+        return jnp.transpose(jnp.broadcast_to(row, (half, half)))
+
+    own_valid = [column(part, tower) for part in range(4)]
+    other_valid = [column(part, 1 - tower) for part in range(4)]
+    row_at = lax.broadcasted_iota(jnp.int32, (half, half), 0)
+    col_at = lax.broadcasted_iota(jnp.int32, (half, half), 1)
+    for part in range(3):
+        where = slice(part * half, (part + 1) * half)
+        distance = col_at + half - (row_at + part * half)
+        for tile in range(2):
+            near = (jnp.abs(distance) <= half) & (own_valid[tile + part] > 0)
+            add = jnp.where(near, 0.0, -1e30)
+            bias[tile, where, :half] = add
+            bias[tile, where, half:] = add
+        at = row_at + part * half + cross_at
+        valid = jnp.where(below, other_valid[part], other_valid[part + 1])
+        inside = (at >= band_low) & (at < band_low + 2 * half) & (valid > 0)
+        add = jnp.where(inside, 0.0, -1e30)
+        bias[2, where, :half] = add
+        bias[2, where, half:] = add
+
+    lanes = lax.broadcasted_iota(jnp.int32, (half, wide), 1)
+    zero = jnp.zeros((half, wide), BF16)
+    zero_half = jnp.zeros((half, wide), F32)
+
+    def split(tile):
+        return jnp.concatenate(
+            (jnp.where(lanes < HEAD, tile, zero), jnp.where(lanes < HEAD, zero, tile)), 0
+        )
+
+    def dot_t(a, b):
+        return lax.dot_general(a, b, (((1,), (1,)), ((), ())), preferred_element_type=F32)
+
+    def dot(a, b):
+        return jnp.dot(a, b, preferred_element_type=F32)
+
+    def own_heads(both):
+        return jnp.concatenate((both[:HEAD, :half], both[HEAD:, half:]), 0)
+
+    def turned(x):
+        return jnp.transpose(x.astype(F32)).astype(BF16)
+
+    def one(query, cot, key, value, key_t, value_t, add):
+        scores = dot_t(key, query) + bias[add]
+        unnormed = jnp.exp(scores - jnp.max(scores, axis=0, keepdims=True))
+        weights = unnormed * (1.0 / jnp.sum(unnormed, axis=0, keepdims=True))
+        prob = weights.astype(BF16)
+        grad_probs = dot_t(value, cot)
+        row_dot = jnp.sum(weights * grad_probs, axis=0, keepdims=True)
+        grad_scores = (weights * (grad_probs - row_dot)).astype(BF16)
+        result = own_heads(dot(value_t, prob))
+        grad_query = own_heads(dot(key_t, grad_scores)) * scale
+        return result, grad_query, dot(grad_scores, query), dot(prob, cot)
+
+    def compute(g):
+        at = strip(g)
+        key, value = ext[0, :, at], ext[1, :, at]
+        ckey = jnp.where(below, ext[2, :keys, at], ext[2, half:, at])
+        cvalue = jnp.where(below, ext[3, :keys, at], ext[3, half:, at])
+        key_t, value_t, ckey_t, cvalue_t = turned(key), turned(value), turned(ckey), turned(cvalue)
+        grad_parts, head_parts = [], []
+        for tile in range(2):
+            span = slice(tile * half, tile * half + keys)
+            part = slice(tile * half, (tile + 1) * half)
+            cot = split(side[2, part, at])
+            query = split(side[0, part, at] * BF16(scale))
+            cross = split(side[1, part, at] * BF16(scale))
+            so, sq, sk, sv = one(
+                query, cot, key[span], value[span], key_t[:, span], value_t[:, span], tile
+            )
+            co, cq, ck, cv = one(cross, cot, ckey, cvalue, ckey_t, cvalue_t, 2)
+            head_parts.append((so + co, sq, cq))
+            grad_parts.append((sk, sv, ck, cv))
+        for i in range(2):
+            first, second = grad_parts[0][i], grad_parts[1][i]
+            low_stage[i, :, at] = first[:half].astype(BF16)
+            core[i, 0, :, at] = first[half : 2 * half] + second[:half]
+            core[i, 1, :, at] = first[2 * half :] + second[half : 2 * half]
+            high_stage[i, :, at] = second[2 * half :].astype(BF16)
+        for i in range(2, 4):
+            total = grad_parts[0][i] + grad_parts[1][i]
+            a, b, c = total[:half], total[half : 2 * half], total[2 * half :]
+            low_stage[i, :, at] = jnp.where(below, a, zero_half).astype(BF16)
+            core[i, 0, :, at] = jnp.where(below, b, a)
+            core[i, 1, :, at] = jnp.where(below, c, b)
+            high_stage[i, :, at] = jnp.where(below, zero_half, c).astype(BF16)
+        for i in range(3):
+            lower = turned(head_parts[0][i])
+            upper = turned(head_parts[1][i])
+            direct[i][:, strip(g, seq * cols)] = jnp.where(seq == 0, lower, upper)
+            y_stage[i, :, at] = jnp.where(seq == 0, upper, lower)
+
+    def grad_down(g, i):
+        at = strip(g)
+        return remote(
+            low_stage.at[i, :, at], recv.at[1, i, :, at],
+            glow_send.at[g, i], glow_recv.at[g, i], peers["low"],
+        )
+
+    def grad_up(g, i):
+        at = strip(g)
+        return remote(
+            high_stage.at[i, :, at], recv.at[0, i, :, at],
+            ghigh_send.at[g, i], ghigh_recv.at[g, i], peers["high"],
+        )
+
+    def outgoing(g):
+        at, to_at = strip(g), strip(g, seq * cols)
+        moves = [(y_stage.at[i, :, at], direct[i].at[:, to_at], "y") for i in range(3)]
+        moves += [
+            (y_stage.at[3 + i, :, at], grads[i].at[:, to_at], "y" if i < 2 else "diag")
+            for i in range(4)
+        ]
+        moves += [(t_stage.at[i, :, at], grads[2 + i].at[:, to_at], "tower") for i in range(2)]
+        return [
+            remote(src, dst, out_send.at[g, i], out_recv.at[g, i], peers[to])
+            for i, (src, dst, to) in enumerate(moves)
+        ]
+
+    def start_down(g):
+        @pl.when(has_low)
+        def _():
+            for i in range(4):
+                grad_down(g, i).start()
+
+    def start_up(g):
+        @pl.when(has_high)
+        def _():
+            for i in range(4):
+                grad_up(g, i).start()
+
+    def give(g):
+        @pl.when(seq == 0)
+        def _():
+            start_down(g)
+            start_up(g)
+
+        @pl.when(seq == 1)
+        def _():
+            start_up(g)
+            start_down(g)
+
+        for copy in outgoing(g)[:3]:
+            copy.start()
+
+    def finish(g):
+        at = strip(g)
+        moves = outgoing(g)
+
+        def take(low_side, high_side, i):
+            @pl.when(low_side & has_low)
+            def _():
+                grad_up(g, i).wait_recv()
+
+            @pl.when(high_side & has_high)
+            def _():
+                grad_down(g, i).wait_recv()
+
+        for i in range(4):
+            take(seq == 1, seq == 0, i)
+            y_stage[3 + i, :, at] = (
+                core[i, 1 - seq, :, at] + recv[1 - seq, i, :, at].astype(F32)
+            ).astype(BF16)
+            moves[3 + i].start()
+        for i in (2, 3, 0, 1):
+            take(seq == 0, seq == 1, i)
+            total = (core[i, seq, :, at] + recv[seq, i, :, at].astype(F32)).astype(BF16)
+            if i < 2:
+                grads[i][:, strip(g, seq * cols)] = total
+            else:
+                t_stage[i - 2, :, at] = total
+                moves[5 + i].start()
+
+    def step(g, carry):
+        @pl.when(g + 1 < groups)
+        def _():
+            pass_on(g + 1, False)
+
+        @pl.when(g + 2 < groups)
+        def _():
+            pass_on(g + 2, True)
+
+        for copy in incoming(g)[6:]:
+            copy.wait_recv()
+
+        @pl.when(has_high)
+        def _():
+            for i in range(4):
+                down(g, i).wait_recv()
+
+        @pl.when(has_low)
+        def _():
+            for i in range(4):
+                up(g, i).wait_recv()
+
+        compute(g)
+        give(g)
+
+        @pl.when(g > 0)
+        def _():
+            finish(g - 1)
+
+        return carry
+
+    lax.fori_loop(0, groups, step, 0)
+    finish(groups - 1)
+
+    def close(g, carry):
+        for copy in incoming(g):
+            copy.wait_send()
+        for copy in outgoing(g):
+            copy.wait()
+
+        @pl.when(has_high)
+        def _():
+            for i in range(4):
+                up(g, i).wait_send()
+                grad_up(g, i).wait_send()
+
+        @pl.when(has_low)
+        def _():
+            for i in range(4):
+                down(g, i).wait_send()
+                grad_down(g, i).wait_send()
+
+        return carry
+
+    lax.fori_loop(0, groups, close, 0)
+    mask_y.wait_send()
+
+    @pl.when(has_high)
+    def _():
+        mask_up.wait_send()
+
+    @pl.when(has_low)
+    def _():
+        mask_down.wait_send()
+
+
+def copy_kernel(*refs):
+    count = len(refs) // 2
+    for src, dst in zip(refs[:count], refs[count:]):
+        dst[...] = src[...]
+
+
+def paired(
+    queries, key_rows, value_rows, cross_queries, cross_keys, cross_values, grad_out,
+    offsets, key_valid,
+):
+    blks = lax.axis_size("blk")
+    cols = HEADS // lax.axis_size("seq") * HEAD
+    values = [
+        value[0] for value in (
+            queries, key_rows, value_rows, cross_queries, cross_keys, cross_values, grad_out
+        )
+    ]
+    rows = queries.shape[1]
+    block, groups = 2 * rows, cols // (2 * HEAD)
+    vmem = pl.BlockSpec(memory_space=pltpu.VMEM)
+    dma = pltpu.SemaphoreType.DMA
+    full = jax.ShapeDtypeStruct((rows, 2 * cols), BF16)
+    outs = pl.pallas_call(
+        functools.partial(fused_kernel, blks, rows, cols),
+        out_shape=(full,) * 7,
+        in_specs=[pl.BlockSpec(memory_space=pltpu.SMEM)] + [pl.BlockSpec(memory_space=pl.ANY)] * 8,
+        out_specs=(vmem,) * 7,
+        scratch_shapes=[
+            pltpu.VMEM((3, block, cols), BF16),
+            pltpu.VMEM((4, 2 * block, cols), BF16),
+            pltpu.VMEM((4,) + key_valid.shape, jnp.int32),
+            pltpu.VMEM((3, 3 * rows, block), F32),
+            pltpu.VMEM((7, rows, cols), BF16),
+            pltpu.VMEM((2, rows, cols), BF16),
+            pltpu.VMEM((4, rows, cols), BF16),
+            pltpu.VMEM((4, rows, cols), BF16),
+            pltpu.VMEM((4, 2, rows, cols), F32),
+            pltpu.VMEM((2, 4, rows, cols), BF16),
+            dma((6,)), dma((3,)), dma((3,)),
+            dma((groups, 9)), dma((groups, 9)),
+            dma((groups, 4)), dma((groups, 4)), dma((groups, 4)), dma((groups, 4)),
+            dma((groups, 9)), dma((groups, 9)),
+            dma((groups, 4)), dma((groups, 4)), dma((groups, 4)), dma((groups, 4)),
+        ],
+        compiler_params=pltpu.CompilerParams(collective_id=0, has_side_effects=True),
+        name="attend_pairs",
+    )(offsets, *values, key_valid)
+    outs = pl.pallas_call(
+        copy_kernel,
+        out_shape=(full,) * 7,
+        in_specs=[vmem] * 7,
+        out_specs=(vmem,) * 7,
+        name="hand_over",
+    )(*outs)
+    return tuple(piece[None] for piece in outs)
 
 
 def extended(block, sides, width):
@@ -237,4 +721,5 @@
         P("tower", ("blk", "seq"), None),
         P("tower", ("blk", "seq"), None),
     )
-    return jax.shard_map(shards, mesh=mesh, in_specs=in_specs, out_specs=out_specs, check_vma=False)
+    body = paired if mesh.shape["seq"] == 2 else shards
+    return jax.shard_map(body, mesh=mesh, in_specs=in_specs, out_specs=out_specs, check_vma=False)

time: 237 us -> 75.9 us (0.32)
  the two profiles are of different devices: /device:TPU:12 before, /device:TPU:17 now
where the time goes in v2:
time: 75.9 us; the launch traced here: 75.8 us
  Pallas kernels  75.1 us (99%)
    pallas_call x1, Pallas kernels, paired(): pl.pallas_call(functools.partial(fused_kernel, blks, rows, cols), out_sha...  72.4 us
    pallas_call x1, Pallas kernels, paired(): pl.pallas_call(copy_kernel, out_shape=(full,) * 7, in_specs=[vmem] * 7, o...  2.67 us

profile of v2, /device:TPU:17, one launch (start us, length us, event | category | flops | bytes accessed | tf_op | source)
XLA Modules:
  0.0 75.8 jit_solution(7229155807820786078)
XLA Ops:
  0.6 72.4 %attend_pairs.1 = (bf16[128,1024]{1,0:T(8,128)(2,1)}, bf16[128,1024]{1,0:T(8,128)(2,1)}, bf16[128,1024]{1,0:T(8,128)(2,1)}, bf16[128,1024]{1,0:T(8,128)(2,1)}, b...) custom-call(s32[2,8]{1,0:T(2,128)} %off_ref.1, bf16[128,1024]{1,0:T(8,128)(2,1)} %bitcast.14, ...), custom_call_target="tpu_custom_call" | custom-call | tf_op jit(solution)/shard_map/attend_pairs/pallas_call | solution.py:461
  73.1 2.7 %hand_over.1 = (bf16[128,1024]{1,0:T(8,128)(2,1)}, bf16[128,1024]{1,0:T(8,128)(2,1)}, bf16[128,1024]{1,0:T(8,128)(2,1)}, bf16[128,1024]{1,0:T(8,128)(2,1)}, bf16...) custom-call(bf16[128,1024]{1,0:T(8,128)(2,1)} %get-tuple-element.21.refs_0_, ...), custom_call_target="tpu_custom_call" | custom-call | tf_op jit(solution)/shard_map/hand_over/pallas_call | solution.py:486

commit v3 on v2

--- a/solution.py
+++ b/solution.py
@@ -156,13 +156,12 @@
 
     greet(blk, blks, peers)
     mask_y.start()
-    for g in range(groups + 1):
-        if g < groups:
-            for copy in incoming(g)[:6]:
-                copy.start()
-        if g > 0:
-            for copy in incoming(g - 1)[6:]:
-                copy.start()
+    for g in range(groups):
+        for copy in incoming(g)[:6]:
+            copy.start()
+    for g in range(groups):
+        for copy in incoming(g)[6:]:
+            copy.start()
     for copy in locals_:
         copy.wait()
     pass_on(0, True)
@@ -176,9 +175,10 @@
     def _():
         mask_down.start()
 
-    pass_on(0, False)
-    if groups > 1:
-        pass_on(1, True)
+    for g in range(1, groups):
+        pass_on(g, True)
+    for g in range(groups):
+        pass_on(g, False)
 
     @pl.when(has_high)
     def _():
@@ -371,14 +371,6 @@
                 moves[5 + i].start()
 
     def step(g, carry):
-        @pl.when(g + 1 < groups)
-        def _():
-            pass_on(g + 1, False)
-
-        @pl.when(g + 2 < groups)
-        def _():
-            pass_on(g + 2, True)
-
         for copy in incoming(g)[6:]:
             copy.wait_recv()
 
@@ -395,14 +387,11 @@
         compute(g)
         give(g)
 
-        @pl.when(g > 0)
-        def _():
-            finish(g - 1)
-
         return carry
 
     lax.fori_loop(0, groups, step, 0)
-    finish(groups - 1)
+    for g in range(groups):
+        finish(g)
 
     def close(g, carry):
         for copy in incoming(g):

time: 75.9 us -> 61.2 us (0.81)
  Pallas kernels: 75.1 us -> 60.4 us
    pallas_call x1, Pallas kernels: 72.4 us -> 57.8 us  [paired(): pl.pallas_call(functools.partial(fused_kernel, blks, rows, cols), out_sha...]
where the time goes in v3:
time: 61.2 us; the launch traced here: 61.1 us
  Pallas kernels  60.4 us (99%)
  between operations  0.64 us (1%)
    pallas_call x1, Pallas kernels, paired(): pl.pallas_call(functools.partial(fused_kernel, blks, rows, cols), out_sha...  57.8 us
    pallas_call x1, Pallas kernels, paired(): pl.pallas_call(copy_kernel, out_shape=(full,) * 7, in_specs=[vmem] * 7, o...  2.67 us

profile of v3, /device:TPU:17, one launch (start us, length us, event | category | flops | bytes accessed | tf_op | source)
XLA Modules:
  0.0 61.1 jit_solution(14575381427242455293)
XLA Ops:
  0.6 57.8 %attend_pairs.1 = (bf16[128,1024]{1,0:T(8,128)(2,1)}, bf16[128,1024]{1,0:T(8,128)(2,1)}, bf16[128,1024]{1,0:T(8,128)(2,1)}, bf16[128,1024]{1,0:T(8,128)(2,1)}, b...) custom-call(s32[2,8]{1,0:T(2,128)} %off_ref.1, bf16[128,1024]{1,0:T(8,128)(2,1)} %bitcast.14, ...), custom_call_target="tpu_custom_call" | custom-call | tf_op jit(solution)/shard_map/attend_pairs/pallas_call | solution.py:450
  58.4 2.7 %hand_over.1 = (bf16[128,1024]{1,0:T(8,128)(2,1)}, bf16[128,1024]{1,0:T(8,128)(2,1)}, bf16[128,1024]{1,0:T(8,128)(2,1)}, bf16[128,1024]{1,0:T(8,128)(2,1)}, bf16...) custom-call(bf16[128,1024]{1,0:T(8,128)(2,1)} %get-tuple-element.21.refs_0_, ...), custom_call_target="tpu_custom_call" | custom-call | tf_op jit(solution)/shard_map/hand_over/pallas_call | solution.py:475

commit v4 on v3

--- a/solution.py
+++ b/solution.py
@@ -98,14 +98,14 @@
     def up(g, i):
         at = strip(g)
         return remote(
-            ext.at[i, inner_high, at], ext.at[i, outer_low, at],
+            ext.at[pl.ds(2 * i, 2), inner_high, at], ext.at[pl.ds(2 * i, 2), outer_low, at],
             high_send.at[g, i], high_recv.at[g, i], peers["high"],
         )
 
     def down(g, i):
         at = strip(g)
         return remote(
-            ext.at[i, inner_low, at], ext.at[i, outer_high, at],
+            ext.at[pl.ds(2 * i, 2), inner_low, at], ext.at[pl.ds(2 * i, 2), outer_high, at],
             low_send.at[g, i], low_recv.at[g, i], peers["low"],
         )
 
@@ -117,11 +117,13 @@
         moved = incoming(g)
         to_high = (seq == 1) if own else (seq == 0)
         to_low = (seq == 0) if own else (seq == 1)
-        for i in range(4):
+        for i in range(2):
             if not own:
-                moved[i].wait_recv()
-            elif i >= 2:
-                moved[i + 2].wait_recv()
+                moved[2 * i].wait_recv()
+                moved[2 * i + 1].wait_recv()
+            elif i == 1:
+                moved[4].wait_recv()
+                moved[5].wait_recv()
 
             @pl.when(to_high & has_high)
             def _():
@@ -376,12 +378,12 @@
 
         @pl.when(has_high)
         def _():
-            for i in range(4):
+            for i in range(2):
                 down(g, i).wait_recv()
 
         @pl.when(has_low)
         def _():
-            for i in range(4):
+            for i in range(2):
                 up(g, i).wait_recv()
 
         compute(g)
@@ -401,14 +403,16 @@
 
         @pl.when(has_high)
         def _():
+            for i in range(2):
+                up(g, i).wait_send()
             for i in range(4):
-                up(g, i).wait_send()
                 grad_up(g, i).wait_send()
 
         @pl.when(has_low)
         def _():
+            for i in range(2):
+                down(g, i).wait_send()
             for i in range(4):
-                down(g, i).wait_send()
                 grad_down(g, i).wait_send()
 
         return carry

time: 61.2 us -> 61.2 us (level)
  no operation moved by 1% of the time
where the time goes in v4:
time: 61.2 us; the launch traced here: 61.1 us
  Pallas kernels  60.4 us (99%)
  between operations  0.64 us (1%)
    pallas_call x1, Pallas kernels, paired(): pl.pallas_call(functools.partial(fused_kernel, blks, rows, cols), out_sha...  57.8 us
    pallas_call x1, Pallas kernels, paired(): pl.pallas_call(copy_kernel, out_shape=(full,) * 7, in_specs=[vmem] * 7, o...  2.67 us

profile of v4, /device:TPU:17, one launch (start us, length us, event | category | flops | bytes accessed | tf_op | source)
XLA Modules:
  0.0 61.1 jit_solution(7740982826109588638)
XLA Ops:
  0.6 57.8 %attend_pairs.1 = (bf16[128,1024]{1,0:T(8,128)(2,1)}, bf16[128,1024]{1,0:T(8,128)(2,1)}, bf16[128,1024]{1,0:T(8,128)(2,1)}, bf16[128,1024]{1,0:T(8,128)(2,1)}, b...) custom-call(s32[2,8]{1,0:T(2,128)} %off_ref.1, bf16[128,1024]{1,0:T(8,128)(2,1)} %bitcast.14, ...), custom_call_target="tpu_custom_call" | custom-call | tf_op jit(solution)/shard_map/attend_pairs/pallas_call | solution.py:454
  58.4 2.7 %hand_over.1 = (bf16[128,1024]{1,0:T(8,128)(2,1)}, bf16[128,1024]{1,0:T(8,128)(2,1)}, bf16[128,1024]{1,0:T(8,128)(2,1)}, bf16[128,1024]{1,0:T(8,128)(2,1)}, bf16...) custom-call(bf16[128,1024]{1,0:T(8,128)(2,1)} %get-tuple-element.21.refs_0_, ...), custom_call_target="tpu_custom_call" | custom-call | tf_op jit(solution)/shard_map/hand_over/pallas_call | solution.py:479
